TPU v7x, 128 devices: a whole 4x4x4 slice. The times are simulated.
128 devices in a mesh: vocab: 128 (over x, z, y, core).
Axes of the slice: x: 4, y: 4, z: 4, core: 2. Of those that a mesh axis runs over, the one named last changes fastest.
Arguments:
- hidden_states: bfloat16 [512, 5120], P('vocab'), may hold values from -8 to 8
- head_weight: bfloat16 [5120, 131072], P(None, 'vocab'), may hold values from -0.25 to 0.25
- teacher_logits: bfloat16 [4, 256, 128, 128], P(None, None, 'vocab'), may hold values from -15 to 260
- block_lists: int32 [4, 256], replicated, may hold values from 0 to 1023, as said below
- row_reader: int32 [4, 128], replicated, may hold values from 0 to 127, each once within a row
- tail_mass: float32 [512], replicated, may hold values from 0.05 to 0.5
- token_weight: float32 [512], replicated, may hold values from 1 to 8
Outputs:
- token_loss: float32 [512], P('vocab')
- grad_head: bfloat16 [5120, 131072], P(None, 'vocab')
- grad_hidden: bfloat16 [512, 5120], P('vocab')
Inputs may be any that keep to these rules, and one draw needn't show every extreme that they name: `block_lists`: for each token block the 256 listed vocabulary blocks are distinct; at most 4 of them lie in any slab of 8 consecutive blocks starting at a multiple of 8, and in every token block some slab holds exactly 4. `row_reader`: each row is a permutation.
All inputs are finite; a program needn't handle non-finite values.
Results may differ from a plain program's by a relative error of at most 0.0048.
Values may be sent and summed in bfloat16 or wider, within the bound.
A program may use at most 128 MiB of HBM per device.

v0:
```python
import jax
import jax.numpy as jnp
from jax import lax
from jax.sharding import Mesh
from jax.sharding import PartitionSpec as P

MOST = 4
VOCAB = ("vocab_0", "vocab_1", "vocab_2", "vocab_3")


def gathered_once(x, axis):
    leaves = jax.tree.leaves(x)
    sequence = sorted(range(len(leaves)), key=lambda k: -leaves[k].size)
    width = (1, *leaves[sequence[0]].shape)[-1]
    lines = [
        jnp.pad(leaves[k].reshape(-1), (0, -leaves[k].size % width)).reshape(-1, width)
        for k in sequence
    ]
    both, at, found = (lax.all_gather(jnp.concatenate(lines), axis), 0, {})
    for k, line in zip(sequence, lines):
        slab = both[:, at : at + len(line)].reshape(len(both), -1)
        found[k] = slab[:, : leaves[k].size].reshape(-1, *leaves[k].shape)
        at += len(line)
    numbers = iter(range(len(leaves)))
    return jax.tree.map(lambda _: found[next(numbers)], x)


def combined_by_axis(x, axes, combine):
    for axis in axes:
        pieces = gathered_once(x, axis)
        x = jax.tree.map(lambda part: part[0], pieces)
        for k in range(1, lax.axis_size(axis)):
            x = combine(x, jax.tree.map(lambda part: part[k], pieces))
    return x


def combine_stats(left_stats, right_stats):
    student_max = jnp.maximum(left_stats[0], right_stats[0])
    left_scale = jnp.exp(left_stats[0] - student_max)
    right_scale = jnp.exp(right_stats[0] - student_max)
    teacher_max = jnp.maximum(left_stats[2], right_stats[2])
    left_teach = jnp.exp(left_stats[2] - teacher_max)
    right_teach = jnp.exp(right_stats[2] - teacher_max)
    return (
        student_max,
        left_stats[1] * left_scale + right_stats[1] * right_scale,
        teacher_max,
        left_stats[3] * left_teach + right_stats[3] * right_teach,
        left_stats[4] * left_teach + right_stats[4] * right_teach,
        left_stats[5] * left_teach + right_stats[5] * right_teach,
        left_stats[6] + right_stats[6],
        left_stats[7] + right_stats[7],
    )


def row_parts(scores, teacher_slab, listed_mask, student_exp, teacher_exp):
    return (
        jnp.sum(student_exp, axis=(2, 3)),
        jnp.sum(teacher_exp, axis=(2, 3)),
        jnp.sum(teacher_exp * scores, axis=(2, 3)),
        jnp.sum(teacher_exp * teacher_slab, axis=(2, 3)),
        jnp.sum(scores, axis=(2, 3)),
        jnp.sum(jnp.where(listed_mask, scores, 0.0), axis=(2, 3)),
    )


def on_device(
    hidden_states, head_weight, teacher_logits, block_lists, row_reader, tail_mass, token_weight
):
    blocks, listed_count, stored_rows, block_side = teacher_logits.shape
    slab_width = head_weight.shape[1]
    slab_blocks = slab_width // block_side
    devices = lax.axis_size(VOCAB)
    rank_self = lax.axis_index(VOCAB)
    tokens = blocks * block_side
    shard_rows = hidden_states.shape[0]
    gathered = lax.all_gather(hidden_states, VOCAB, axis=0, tiled=True)
    logits = jnp.dot(gathered, head_weight, preferred_element_type=jnp.float32)
    owner_dev = block_lists // slab_blocks
    earlier = lax.broadcasted_iota(
        jnp.int32, (1, listed_count, listed_count), 2
    ) < lax.broadcasted_iota(jnp.int32, (1, listed_count, listed_count), 1)
    same_owner = owner_dev[:, :, None] == owner_dev[:, None, :]
    order_rank = jnp.sum((same_owner & earlier).astype(jnp.int32), axis=2)
    owned_here = owner_dev == rank_self
    within = block_lists - rank_self * slab_blocks
    token_iota = lax.broadcasted_iota(jnp.int32, (1, block_side, block_side), 1)
    token_map = (row_reader[:, None, :] == token_iota).astype(jnp.bfloat16)
    place_iota = lax.broadcasted_iota(jnp.int32, (1, slab_blocks, 1), 1)
    target = owner_dev * MOST + order_rank
    slot_ids = lax.broadcasted_iota(jnp.int32, (1, devices * MOST, 1), 1)
    picker = (target[:, None, :] == slot_ids).astype(jnp.bfloat16)
    outgoing = jnp.einsum(
        "tsk,tkrc->tsrc", picker, teacher_logits, preferred_element_type=jnp.float32
    ).astype(jnp.bfloat16)
    incoming = lax.all_to_all(outgoing, VOCAB, split_axis=1, concat_axis=2, tiled=True)
    ordered = jnp.einsum(
        "tpj,tmjc->tmpc", token_map, incoming, preferred_element_type=jnp.float32
    ).astype(jnp.bfloat16)
    rank_iota = lax.broadcasted_iota(jnp.int32, (1, MOST, 1, 1), 1)
    hits = (
        owned_here[:, None, None, :]
        & (order_rank[:, None, None, :] == rank_iota)
        & (within[:, None, None, :] == place_iota[:, None, :, :])
    )
    choose = jnp.sum(hits.astype(jnp.int32), axis=3)
    teacher_slab = jnp.einsum(
        "tmb,tmpc->tpbc", choose.astype(jnp.bfloat16), ordered, preferred_element_type=jnp.float32
    )
    listed = jnp.sum(choose, axis=1)
    scores = logits.reshape(blocks, block_side, slab_blocks, block_side)
    listed_mask = (listed > 0)[:, None, :, None]
    local_smax = jnp.max(scores, axis=(2, 3))
    local_tmax = jnp.max(jnp.where(listed_mask, teacher_slab, -1e30), axis=(2, 3))
    local_sexp = jnp.exp(scores - local_smax[:, :, None, None])
    local_texp = jnp.exp(
        jnp.where(listed_mask, teacher_slab - local_tmax[:, :, None, None], -jnp.inf)
    )
    parts = row_parts(scores, teacher_slab, listed_mask, local_sexp, local_texp)
    merged = combined_by_axis(
        (local_smax, parts[0], local_tmax, parts[1], parts[2], parts[3], parts[4], parts[5]),
        VOCAB,
        combine_stats,
    )
    (
        student_max,
        student_sum,
        teacher_max,
        teacher_sum,
        cross_sum,
        self_sum,
        logit_total,
        listed_total,
    ) = merged
    student_exp = jnp.exp(scores - student_max[:, :, None, None])
    teacher_exp = jnp.exp(
        jnp.where(listed_mask, teacher_slab - teacher_max[:, :, None, None], -jnp.inf)
    )
    tail_share = tail_mass.reshape(blocks, block_side)
    unlisted = float(devices * slab_width - block_side * listed_count)
    kept_mass = 1.0 - tail_share
    log_norm = student_max + jnp.log(student_sum)
    row_loss = (
        kept_mass * (jnp.log(kept_mass) - teacher_max - jnp.log(teacher_sum))
        + kept_mass * self_sum / teacher_sum
        + tail_share * jnp.log(tail_share / unlisted)
        - kept_mass * cross_sum / teacher_sum
        - tail_share / unlisted * (logit_total - listed_total)
        + log_norm
    )
    token_loss = lax.dynamic_slice_in_dim(
        row_loss.reshape(tokens), rank_self * shard_rows, shard_rows, 0
    )
    student_prob = student_exp / student_sum[:, :, None, None]
    teacher_prob = jnp.where(
        listed_mask,
        (kept_mass / teacher_sum)[:, :, None, None] * teacher_exp,
        (tail_share / unlisted)[:, :, None, None],
    )
    weight = token_weight.reshape(blocks, block_side)[:, :, None, None]
    grad_logits = (
        (weight * (student_prob - teacher_prob)).astype(jnp.bfloat16).reshape(tokens, slab_width)
    )
    grad_head = lax.dot_general(
        gathered, grad_logits, (((0,), (0,)), ((), ())), preferred_element_type=jnp.float32
    ).astype(jnp.bfloat16)
    grad_hidden = lax.psum_scatter(
        lax.dot_general(
            grad_logits, head_weight, (((1,), (1,)), ((), ())), preferred_element_type=jnp.float32
        ),
        VOCAB,
        scatter_dimension=0,
        tiled=True,
    ).astype(jnp.bfloat16)
    return (token_loss, grad_head, grad_hidden)


def solution(mesh):
    split = Mesh(mesh.devices.reshape(4, 4, 4, 2), ("vocab_0", "vocab_1", "vocab_2", "vocab_3"))
    return jax.shard_map(
        on_device,
        mesh=split,
        in_specs=(P(VOCAB, None), P(None, VOCAB), P(None, None, VOCAB, None), P(), P(), P(), P()),
        out_specs=(P(VOCAB), P(None, VOCAB), P(VOCAB, None)),
        check_vma=False,
    )
```

profile of v0, /device:TPU:0, one launch (start us, length us, event | category | flops | bytes accessed | tf_op | source)
XLA Modules:
  0.0 317.0 jit_solution(2357829539890584598)
XLA Ops:
  7.2 0.0 copy-start
  7.2 0.0 copy-start.3
  7.2 0.0 all-gather.7.cloned.1.call-start
  7.2 0.7 all-gather.7.cloned.1.call-update
  8.0 0.7 broadcast_compare_fusion
  8.7 0.4 convert_reduce_fusion
  9.1 0.0 copy-done
  9.1 0.0 copy-start.5
  9.1 0.5 fusion.18
  9.6 1.2 copy.16
  10.8 11.2 %all-to-all-start = ((bf16[4,512,1,128]{3,0,2,1:T(4,128)(2,1)}), bf16[4,512,1,128]{3,0,2,1:T(4,128)(2,1)S(1)}, u32[]{:S(2)}, u32[]{:S(2)}) async-start(bf16[4,512,1,128]{3,0,2,1:T(4,128)(2,1)} %copy.16), calls=%async_computation | async-start | bytes 1048576 | tf_op jit(solution)/shard_map/all_to_all | solution.py:96
  22.0 0.0 copy-done.3
  22.0 0.4 convert_reduce_fusion.2
  22.5 13.2 %all-to-all-done = bf16[4,512,1,128]{3,0,2,1:T(4,128)(2,1)S(1)} async-done(((bf16[4,512,1,128]{3,0,2,1:T(4,128)(2,1)}), bf16[4,512,1,128]{3,0,2,1:T(4,128)(2,1)S(1)}, u32[]{:S(2)}, u32[]{:S(2)}) %all-to-all-start) | async-done | bytes 524320 | tf_op jit(solution)/shard_map/all_to_all | solution.py:96
  35.7 0.5 copy.18
  36.1 0.0 copy-done.5
  36.1 0.3 fusion.17
  36.5 0.3 copy.19
  36.8 1.6 fusion.5
  38.4 43.9 %all-gather.7.cloned.1.call-done = bf16[128,4,5120]{2,1,0:T(4,128)(2,1)} async-done(((bf16[1,4,5120]{2,1,0:T(4,128)(2,1)}), bf16[128,4,5120]{2,1,0:T(4,128)(2,1)}) %all-gather.7.cloned.1.call-update) | async-done | bytes 5242896 | tf_op jit(solution)/shard_map/all_gather | solution.py:77
  82.3 8.9 %reshape.262 = bf16[512,5120]{1,0:T(8,128)(2,1)} reshape(bf16[128,4,5120]{2,1,0:T(4,128)(2,1)} %all-gather.7.cloned.1.call-done) | data formatting | bytes 10485760
  91.2 10.0 %fusion.209 = (f32[512]{0:T(512)S(1)}, f32[512,1024]{1,0:T(8,128)S(1)}) fusion(bf16[512,5120]{1,0:T(8,128)(2,1)} %reshape.262, bf16[5120,1024]{1,0:T(8,128)(2,1)} %param.8), kind=kOutput, calls=%fused_computation.360 | convolution fusion | flops 5369232896 | bytes 17827840 | tf_op jit(solution)/shard_map/dot_general | solution.py:78
  101.2 0.5 copy.25
  101.7 0.0 copy-start.2
  101.7 0.2 broadcast_in_dim.59
  101.9 0.8 select_reduce_fusion
  102.7 0.0 copy-start.4
  102.7 0.0 copy-start.6
  102.7 9.0 %fusion.9 = (f32[4,128]{1,0:T(4,128)S(1)}, f32[4,128]{1,0:T(4,128)S(1)}, f32[4,128]{1,0:T(4,128)S(1)}) fusion(f32[4,128,128,8]{2,3,1,0:T(8,128)S(1)} %get-tuple-element.69, f32[4,128]{1,0:T(4,128)S(1)} %get-tuple-element.68, pred[4,8]{1,0:T(4,128)(4,1)S(1)} %broadcast_compare_fusion.1, f32[4,128,8,128]{3,2,1,0:T(8,128)S(1)} %bitcast.967), kind=kLoop, calls=%fused_computation.16 | loop fusion | flops 3668480 | bytes 4202528 | tf_op jit(solution)/shard_map/reduce_sum | solution.py:61
  111.8 0.0 copy-done.2
  111.8 0.1 concatenate.12
  111.9 11.9 %all-gather = f32[128,128]{1,0:T(8,128)S(1)} all-gather(f32[32,128]{1,0:T(8,128)S(1)} %concatenate.12), channel_id=2, replica_groups=mesh['vocab_0'=4,'vocab_1'=4,'vocab_2'=4,'vocab_3'=2] {'vocab_0'}, dimensions={0}, use_global_device_ids=true | all-gather | bytes 81920 | tf_op jit(solution)/shard_map/all_gather | solution.py:19
  123.8 0.1 concatenate.13
  123.9 11.9 %all-gather.1 = f32[128,128]{1,0:T(8,128)S(1)} all-gather(f32[32,128]{1,0:T(8,128)S(1)} %concatenate.13), channel_id=3, replica_groups=mesh['vocab_0'=4,'vocab_1'=4,'vocab_2'=4,'vocab_3'=2] {'vocab_1'}, dimensions={0}, use_global_device_ids=true | all-gather | bytes 81920 | tf_op jit(solution)/shard_map/all_gather | solution.py:19
  135.8 0.1 concatenate.14
  135.9 12.0 %all-gather.2 = f32[128,128]{1,0:T(8,128)S(1)} all-gather(f32[32,128]{1,0:T(8,128)S(1)} %concatenate.14), channel_id=4, replica_groups=mesh['vocab_0'=4,'vocab_1'=4,'vocab_2'=4,'vocab_3'=2] {'vocab_2'}, dimensions={0}, use_global_device_ids=true | all-gather | bytes 81920 | tf_op jit(solution)/shard_map/all_gather | solution.py:19
  148.0 0.1 concatenate.15
  148.1 1.8 all-gather.3
  149.9 0.0 copy-done.4
  149.9 0.0 copy-done.6
  149.9 0.0 slice-start
  150.0 6.5 %fusion.14 = bf16[4,128,8,128]{3,2,1,0:T(8,128)(2,1)S(1)} fusion(f32[4,128,128,8]{2,3,1,0:T(8,128)S(1)} %get-tuple-element.69, f32[4,128]{1,0:T(4,128)S(1)} %get-tuple-element.64, f32[4,128]{1,0:T(4,128)S(1)} %get-tuple-element.63, f32[4,128]{1,0:T(4,128)S(1)} %get-tuple-element.62, f32[4,128]{1,0:T(4,128)S(1)} %get-tuple-element.23, ...), kind=kLoop, calls=%fused_computation.24 | loop fusion | flops 4718592 | bytes 5255200 | tf_op jit(solution)/shard_map/convert_element_type | solution.py:162
  156.5 0.0 slice-start.1
  156.5 12.3 %fusion.19 = f32[512,5120]{1,0:T(8,128)} fusion(bf16[5120,1024]{1,0:T(8,128)(2,1)} %param.8, bf16[64,8,8,128]{3,2,1,0:T(8,128)(2,1)S(1)} %bitcast.974), kind=kOutput, calls=%fused_computation.30 | convolution fusion | flops 5368709120 | bytes 22020096 | tf_op jit(solution)/shard_map/dot_general | solution.py:168
  168.8 0.0 slice-done
  168.8 0.0 slice-done.1
  168.8 8.3 %convert_bitcast_fusion = bf16[5120,1024]{0,1:T(8,128)(2,1)} fusion(bf16[512,5120]{1,0:T(8,128)(2,1)S(1)} %bitcast.971, bf16[64,8,8,128]{3,2,1,0:T(8,128)(2,1)S(1)} %bitcast.975), kind=kOutput, calls=%fused_computation | convolution fusion | flops 5373952000 | bytes 16777216 | tf_op jit(solution)/shard_map/dot_general | solution.py:164
  177.1 116.5 %all-reduce.2 = bf16[512,5120]{1,0:T(8,128)(2,1)} all-reduce(f32[512,5120]{1,0:T(8,128)} %fusion.19), channel_id=6, replica_groups=mesh['vocab_0'=4,'vocab_1'=4,'vocab_2'=4,'vocab_3'=2] {'vocab_0','vocab_..., use_global_device_ids=true, to_apply=%region_11.12.clone | all-reduce | flops 2621440 | bytes 15728640
  293.6 0.0 copy-start.1
  293.6 14.4 %copy.20 = bf16[5120,1024]{1,0:T(8,128)(2,1)} copy(bf16[5120,1024]{0,1:T(8,128)(2,1)} %convert_bitcast_fusion) | data formatting | bytes 20971520
  308.0 1.5 dynamic-slice_convert_fusion
  309.5 0.6 dynamic_slice.3
  310.1 0.0 copy-done.1
  (18 shorter events, 0.3 us)
Async XLA Ops:
  7.2 1.9 copy-start
  7.2 14.8 %copy-start.3 = (s32[4,256]{1,0:T(4,128)S(1)}, s32[4,256]{1,0:T(4,128)}, u32[]{:S(2)}) copy-start(s32[4,256]{1,0:T(4,128)} %param.10) | copy-start | bytes 12292
  7.2 75.1 %all-gather.7.cloned.1.call-start = ((), (), s32[]{:S(2)}) async-start(), calls=%async_computation.1 | async-start | bytes 5283840 | tf_op jit(solution)/shard_map/all_gather | solution.py:77
  9.1 27.1 %copy-start.5 = (s32[4,128]{1,0:T(4,128)S(1)}, s32[4,128]{1,0:T(4,128)}, u32[]{:S(2)}) copy-start(s32[4,128]{1,0:T(4,128)} %param.11) | copy-start | bytes 6148
  10.8 24.9 %all-to-all-start = ((bf16[4,512,1,128]{3,0,2,1:T(4,128)(2,1)}), bf16[4,512,1,128]{3,0,2,1:T(4,128)(2,1)S(1)}, u32[]{:S(2)}, u32[]{:S(2)}) async-start(bf16[4,512,1,128]{3,0,2,1:T(4,128)(2,1)} %copy.16), calls=%async_computation | async-start | bytes 1048576 | tf_op jit(solution)/shard_map/all_to_all | solution.py:96
  101.7 10.1 %copy-start.2 = (f32[64,8,8,128]{3,2,1,0:T(8,128)}, f32[64,8,8,128]{3,2,1,0:T(8,128)S(1)}, u32[]{:S(2)}) copy-start(f32[64,8,8,128]{3,2,1,0:T(8,128)S(1)} %copy.25) | copy-start | bytes 6291460
  102.7 47.2 %copy-start.4 = (f32[512]{0:T(512)S(1)}, f32[512]{0:T(512)}, u32[]{:S(2)}) copy-start(f32[512]{0:T(512)} %param.12) | copy-start | bytes 6148
  102.7 47.2 %copy-start.6 = (f32[512]{0:T(512)S(1)}, f32[512]{0:T(512)}, u32[]{:S(2)}) copy-start(f32[512]{0:T(512)} %param.13) | copy-start | bytes 6148
  149.9 18.8 %slice-start = ((s8[5242880]{0:T(1024)(128)(4,1)}), s8[4194304]{0:T(1024)(128)(4,1)S(1)}, s32[]{:S(2)}) async-start(s8[5242880]{0:T(1024)(128)(4,1)} %bitcast.970), calls=%async_computation.2 | async-start | bytes 8388608
  156.5 12.3 %slice-start.1 = ((s8[5242880]{0:T(1024)(128)(4,1)}), s8[1048576]{0:T(1024)(128)(4,1)S(1)}, s32[]{:S(2)}) async-start(s8[5242880]{0:T(1024)(128)(4,1)} %bitcast.970), calls=%async_computation.3 | async-start | bytes 2097152
  293.6 16.5 %copy-start.1 = (bf16[4,256,1,128]{3,1,2,0:T(8,128)(2,1)S(1)}, bf16[4,256,1,128]{3,1,2,0:T(8,128)(2,1)}, u32[]{:S(2)}) copy-start(bf16[4,256,1,128]{3,1,2,0:T(8,128)(2,1)} %param.9) | copy-start | bytes 786436
Sparse Core Ops, SparseCore 0:
  11.0 71.2 all-gather.6
where the time goes:
time: 318 us; the launch traced here: 317 us
  blocking collectives  154 us (48%)
  waiting for transfers between devices  57.8 us (18%)
  matrix products  33 us (10%)
  local copies, waits for them, and re-layouts  28.5 us (9%)
  other arithmetic  18.2 us (6%)
  between operations  14.3 us (4%)
  starting transfers between devices  11.2 us (4%)
    unnamed x1, blocking collectives  116 us
    all_gather x1, waiting for transfers between devices, on_device(): gathered = lax.all_gather(hidden_states, VOCAB, axis=0, tiled=True)  43.9 us
    all_gather x4, blocking collectives, gathered_once(): both, at, found = (lax.all_gather(jnp.concatenate(lines), axis), 0, {})  37.6 us
    unnamed x21, local copies, waits for them, and re-layouts  23.9 us
    all_to_all x1, waiting for transfers between devices, on_device(): lax.all_to_all(outgoing, VOCAB, split_axis=1, concat_axis=2, tiled=True)  13.2 us
    dot_general x1, matrix products, on_device(): lax.dot_general(grad_logits, head_weight, (((1,), (1,)), ((), ())), prefe...  12.3 us
    all_to_all x1, starting transfers between devices, on_device(): lax.all_to_all(outgoing, VOCAB, split_axis=1, concat_axis=2, tiled=True)  11.2 us
    dot_general x1, matrix products, on_device(): logits = jnp.dot(gathered, head_weight, preferred_element_type=jnp.float32)  9.97 us
  transfers between devices with their start and end apart: 2, of which 2 were waited for; matrix products, arithmetic and copies ran while one was open for 2% of the time, Pallas kernels for 0%

commit v1 on v0

v1 whole, which is shorter than its diff:
```python
import functools

import jax
import jax.numpy as jnp
from jax import lax
from jax.experimental import pallas as pl
from jax.experimental.pallas import tpu as pltpu
from jax.sharding import Mesh
from jax.sharding import PartitionSpec as P

MOST = 4
AXES = ("x", "z", "y", "c")
N = 4
D = 5120
CHUNKS = ((0, 1280, "x", "z"), (1280, 1280, "z", "x"), (2560, 1280, "x", "z"), (3840, 1280, "z", "x"))
NC = len(CHUNKS)
DMA = pltpu.SemaphoreType.DMA
REGULAR = pltpu.SemaphoreType.REGULAR
VM = pl.BlockSpec(memory_space=pltpu.VMEM)
ANY = pl.BlockSpec(memory_space=pl.ANY)


def spot():
    return {a: lax.axis_index(a) for a in AXES}


def moved(pos, axis, step):
    if axis == "c":
        return {"c": 1 - pos["c"]}
    return {axis: lax.rem(pos[axis] + step + N, N)}


def remote(src, dst, send, recv, device):
    return pltpu.make_async_remote_copy(
        src_ref=src, dst_ref=dst, send_sem=send, recv_sem=recv,
        device_id=device, device_id_type=pl.DeviceIdType.MESH,
    )


def greet(pos, partners):
    barrier = pltpu.get_barrier_semaphore()
    for device in partners:
        pl.semaphore_signal(barrier, inc=1, device_id=device, device_id_type=pl.DeviceIdType.MESH)
    pl.semaphore_wait(barrier, len(partners))


def lines(pos, axes):
    return [moved(pos, a, s) for a in axes for s in ((1,) if a == "c" else (1, 2, 3))]


def gather_chunk(pos, f, full, asend, arecv, bsend, brecv, csend, crecv):
    start, width, A, B = CHUNKS[f]
    half = width // 2
    a, b, c = pos[A], pos[B], pos["c"]
    every, low, high = pl.ds(start, width), pl.ds(start, half), pl.ds(start + half, half)
    sent = []

    def unit(off_a, off_b, cols):
        at = {A: lax.rem(a + off_a + N, N), B: lax.rem(b + off_b + N, N)}
        return full.at[at["x"], at["z"], c, :, cols]

    def send(ref, send_sem, recv_sem, axis, step):
        copy = remote(ref, ref, send_sem, recv_sem, moved(pos, axis, step))
        copy.start()
        sent.append(copy)

    def arrived(ref, recv_sem):
        remote(ref, ref, recv_sem, recv_sem, moved(pos, "c", 1)).wait_recv()

    offs = (0, -1, 1, 2)

    def onward(j):
        ref = unit(offs[j], 0, every)
        send(ref, bsend.at[f, j, 0], brecv.at[f, j, 0], B, 1)
        send(ref, bsend.at[f, j, 1], brecv.at[f, j, 1], B, -1)
        across(j, 0)

    def across(j, k):
        send(unit(offs[j], offs[k], every), csend.at[f, j, k], crecv.at[f, j, k], "c", 1)

    ref = unit(0, 0, every)
    send(ref, asend.at[f, 0], arecv.at[f, 0], A, 1)
    send(ref, asend.at[f, 1], arecv.at[f, 1], A, -1)
    onward(0)
    yield
    arrived(unit(-1, 0, every), arecv.at[f, 0])
    send(unit(-1, 0, low), asend.at[f, 2], arecv.at[f, 2], A, 1)
    onward(1)
    arrived(unit(1, 0, every), arecv.at[f, 1])
    send(unit(1, 0, high), asend.at[f, 3], arecv.at[f, 3], A, -1)
    onward(2)
    yield

    def relay(j):
        arrived(unit(offs[j], -1, every), brecv.at[f, j, 0])
        send(unit(offs[j], -1, low), bsend.at[f, j, 2], brecv.at[f, j, 2], B, 1)
        across(j, 1)
        arrived(unit(offs[j], 1, every), brecv.at[f, j, 1])
        send(unit(offs[j], 1, high), bsend.at[f, j, 3], brecv.at[f, j, 3], B, -1)
        across(j, 2)

    relay(0)
    yield
    arrived(unit(2, 0, low), arecv.at[f, 2])
    arrived(unit(2, 0, high), arecv.at[f, 3])
    onward(3)
    yield
    relay(1)
    relay(2)
    yield
    relay(3)
    yield
    for j in range(4):
        arrived(unit(offs[j], 2, low), brecv.at[f, j, 2])
        arrived(unit(offs[j], 2, high), brecv.at[f, j, 3])
        across(j, 3)
    yield
    for j in range(4):
        for k in range(4):
            at = {A: lax.rem(a + offs[j] + N, N), B: lax.rem(b + offs[k] + N, N)}
            arrived(full.at[at["x"], at["z"], 1 - c, :, every], crecv.at[f, j, k])
    for copy in sent:
        copy.wait_send()


def run_all(gens):
    gens = list(gens)
    while gens:
        for g in list(gens):
            try:
                next(g)
            except StopIteration:
                gens.remove(g)


def gather_kernel(h_ref, out_ref, full, inc, rows, wide, ysend, yrecv, asend, arecv, bsend, brecv,
                  csend, crecv, tsend, trecv, own, gz, gx, gc):
    pos = spot()
    x, z, y, c = (pos[a] for a in AXES)
    me = ((x * N + z) * N + y) * 2 + c
    greet(pos, lines(pos, AXES))

    def everyone(sem, axes):
        partners = lines(pos, axes)
        for device in partners:
            pl.semaphore_signal(sem, inc=1, device_id=device, device_id_type=pl.DeviceIdType.MESH)
        pl.semaphore_wait(sem, len(partners))

    first = []
    for d in (1, 2, 3):
        copy = remote(h_ref, rows.at[y], ysend.at[d - 1], yrecv.at[d - 1], moved(pos, "y", d))
        copy.start()
        first.append(copy)
    mine = pltpu.make_async_copy(h_ref, rows.at[y], own.at[0])
    mine.start()
    keep = pltpu.make_async_copy(out_ref.at[me], inc.at[me], own.at[1])
    keep.start()
    everyone(gz, ("z",))
    mine.wait()
    for d in (1, 2, 3):
        ref = rows.at[lax.rem(y - d + N, N)]
        remote(ref, ref, ysend.at[d - 1], yrecv.at[d - 1], moved(pos, "y", d)).wait_recv()
    for k in range(N):
        wide[4 * k : 4 * k + 4, :] = rows[k].astype(jnp.float32)
    full[x, z, c] = wide[...].astype(jnp.bfloat16)
    gens = [gather_chunk(pos, f, full, asend, arecv, bsend, brecv, csend, crecv) for f in range(NC)]
    for g in gens:
        next(g)
    everyone(gx, ("x",))
    everyone(gc, ("c",))

    def one(k, carry):
        to = lax.rem(me + k, 128)
        device = {"x": to // 32, "z": lax.rem(to // 8, N), "y": lax.rem(to // 2, N), "c": lax.rem(to, 2)}
        remote(out_ref.at[to], inc.at[me], tsend, trecv, device).start()
        return carry

    lax.fori_loop(1, 128, one, 0)
    run_all(gens)
    for copy in first:
        copy.wait_send()
    part = inc.at[pl.ds(0, 127)]
    remote(part, part, tsend, trecv, moved(pos, "c", 1)).wait()
    keep.wait()


def gather(hidden, outgoing):
    return pl.pallas_call(
        gather_kernel,
        out_shape=(
            jax.ShapeDtypeStruct((N, N, 2, 16, D), jnp.bfloat16),
            jax.ShapeDtypeStruct(outgoing.shape, jnp.bfloat16),
        ),
        in_specs=[VM, VM],
        out_specs=(VM, VM),
        scratch_shapes=[
            pltpu.VMEM((N, 4, D), jnp.bfloat16),
            pltpu.VMEM((16, D), jnp.float32),
            DMA((3,)), DMA((3,)),
            DMA((NC, 4)), DMA((NC, 4)),
            DMA((NC, 4, 4)), DMA((NC, 4, 4)),
            DMA((NC, 4, 4)), DMA((NC, 4, 4)),
            DMA, DMA, DMA((2,)),
            REGULAR, REGULAR, REGULAR,
        ],
        compiler_params=pltpu.CompilerParams(collective_id=0, has_side_effects=True, vmem_limit_bytes=60 << 20),
        name="gather",
    )(hidden, outgoing)


def merge(parts):
    top = parts[0][0]
    for p in parts[1:]:
        top = jnp.maximum(top, p[0])
    row = lax.broadcasted_iota(jnp.int32, (8, 128), 0)
    sums = [0.0, 0.0, 0.0]
    for p in parts:
        scale = jnp.exp(p[0] - top)
        sums[0] += p[1] * scale
        sums[1] += p[2] * jnp.where(row < 4, 1.0, scale)
        sums[2] += p[3] * scale
    return [top] + sums


def stats_kernel(st, out, near, mid, far, send1, recv1, send2, recv2):
    pos = spot()
    x, z, y, c = (pos[a] for a in AXES)
    plane = [{"z": lax.rem(z + dz, N), "y": lax.rem(y + dy, N)} for dz in range(N) for dy in range(N) if dz or dy]
    line = [{"x": lax.rem(x + dx, N), "c": lax.rem(c + dc, 2)} for dx in range(N) for dc in range(2) if dx or dc]
    greet(pos, plane + line)
    for device in plane:
        remote(st, near.at[z * N + y], send1, recv1, device).start()
    near[z * N + y] = st[...]
    group = near.at[pl.ds(0, 15)]
    remote(group, group, send1, recv1, plane[0]).wait()
    for k, v in enumerate(merge([near[i] for i in range(16)])):
        mid[k] = v
    for device in line:
        remote(mid, far.at[x * 2 + c], send2, recv2, device).start()
    far[x * 2 + c] = mid[...]
    group = far.at[pl.ds(0, 7)]
    remote(group, group, send2, recv2, line[0]).wait()
    for k, v in enumerate(merge([far[i] for i in range(8)])):
        out[k] = v


def stats_merge(st):
    return pl.pallas_call(
        stats_kernel,
        out_shape=jax.ShapeDtypeStruct(st.shape, st.dtype),
        in_specs=[VM],
        out_specs=VM,
        scratch_shapes=[
            pltpu.VMEM((16,) + st.shape, st.dtype),
            pltpu.VMEM(st.shape, st.dtype),
            pltpu.VMEM((8,) + st.shape, st.dtype),
            DMA, DMA, DMA, DMA,
        ],
        compiler_params=pltpu.CompilerParams(collective_id=1, has_side_effects=True),
        name="stats_merge",
    )(st)


W = CHUNKS[0][1]
TILE = 256


def scatter_chunk(pos, f, gl, w, part, cs, cr, bs1, br1, bs2, br2, red, as1, ar1, as2, ar2, ys, yr,
                  out, csem, bsem, asem, ysem):
    start, width, A, B = CHUNKS[f]
    half = width // 2
    a, b, c, y = pos[A], pos[B], pos["c"], pos["y"]
    f32, bf16 = jnp.float32, jnp.bfloat16
    sent = []

    def index(ia, ib):
        at = {A: ia, B: ib}
        return at["x"] * N + at["z"]

    def shift(p, s):
        return lax.rem(p + s + N, N)

    def send(src, dst, sems, k, axis, step):
        copy = remote(src, dst, sems.at[0, f, k], sems.at[1, f, k], moved(pos, axis, step))
        copy.start()
        sent.append(copy)

    def arrived(ref, sems, k):
        remote(ref, ref, sems.at[0, f, k], sems.at[1, f, k], moved(pos, "c", 1)).wait_recv()

    def product(i, carry):
        rows = w[pl.ds(pl.multiple_of(start + i * TILE, TILE), TILE), :]
        got = lax.dot_general(gl[...], rows, (((1,), (1,)), ((), ())), preferred_element_type=f32)
        part[f, :, :, :, pl.ds(pl.multiple_of(i * TILE, TILE), TILE)] = got.reshape(16, 2, 16, TILE)
        return carry

    lax.fori_loop(0, width // TILE, product, 0)

    def other(u, carry):
        cs[f, u] = part[f, u, 1 - c].astype(bf16)
        return carry

    lax.fori_loop(0, 16, other, 0)
    send(cs.at[f], cr.at[f], csem, 0, "c", 1)
    yield
    arrived(cr.at[f], csem, 0)

    def chip(u):
        return part[f, u, c] + cr[f, u].astype(f32)

    def opposite(i, carry):
        v = chip(index(i, shift(b, 2))).astype(bf16)
        bs1[f, 0, i] = v[:, :half]
        bs1[f, 1, i] = v[:, half:]
        return carry

    lax.fori_loop(0, N, opposite, 0)
    send(bs1.at[f, 0], br1.at[f, 0], bsem, 0, B, 1)
    send(bs1.at[f, 1], br1.at[f, 1], bsem, 1, B, -1)
    yield
    arrived(br1.at[f, 0], bsem, 0)

    def up(i, carry):
        v = chip(index(i, shift(b, 1)))
        bs2[f, 0, i, :, :half] = (v[:, :half] + br1[f, 0, i].astype(f32)).astype(bf16)
        bs2[f, 0, i, :, half:] = v[:, half:].astype(bf16)
        return carry

    lax.fori_loop(0, N, up, 0)
    send(bs2.at[f, 0], br2.at[f, 0], bsem, 2, B, 1)
    arrived(br1.at[f, 1], bsem, 1)

    def down(i, carry):
        v = chip(index(i, shift(b, -1)))
        bs2[f, 1, i, :, :half] = v[:, :half].astype(bf16)
        bs2[f, 1, i, :, half:] = (v[:, half:] + br1[f, 1, i].astype(f32)).astype(bf16)
        return carry

    lax.fori_loop(0, N, down, 0)
    send(bs2.at[f, 1], br2.at[f, 1], bsem, 3, B, -1)
    yield
    arrived(br2.at[f, 0], bsem, 2)
    arrived(br2.at[f, 1], bsem, 3)

    def kept(i, carry):
        red[f, i] = chip(index(i, b)) + br2[f, 0, i].astype(f32) + br2[f, 1, i].astype(f32)
        return carry

    lax.fori_loop(0, N, kept, 0)
    v = red[f, shift(a, 2)].astype(bf16)
    as1[f, 0] = v[:, :half]
    as1[f, 1] = v[:, half:]
    send(as1.at[f, 0], ar1.at[f, 0], asem, 0, A, 1)
    send(as1.at[f, 1], ar1.at[f, 1], asem, 1, A, -1)
    yield
    arrived(ar1.at[f, 0], asem, 0)
    v = red[f, shift(a, 1)]
    as2[f, 0, :, :half] = (v[:, :half] + ar1[f, 0].astype(f32)).astype(bf16)
    as2[f, 0, :, half:] = v[:, half:].astype(bf16)
    send(as2.at[f, 0], ar2.at[f, 0], asem, 2, A, 1)
    arrived(ar1.at[f, 1], asem, 1)
    v = red[f, shift(a, -1)]
    as2[f, 1, :, :half] = v[:, :half].astype(bf16)
    as2[f, 1, :, half:] = (v[:, half:] + ar1[f, 1].astype(f32)).astype(bf16)
    send(as2.at[f, 1], ar2.at[f, 1], asem, 3, A, -1)
    yield
    arrived(ar2.at[f, 0], asem, 2)
    arrived(ar2.at[f, 1], asem, 3)
    v = red[f, a] + ar2[f, 0].astype(f32) + ar2[f, 1].astype(f32)
    for k in range(N):
        ys[f, k] = v[4 * k : 4 * k + 4, :]
    for d in (1, 2, 3):
        send(ys.at[f, shift(y, d)], yr.at[f, d - 1], ysem, d - 1, "y", d)
    yield
    for d in (1, 2, 3):
        arrived(yr.at[f, d - 1], ysem, d - 1)
    total = ys[f, y] + yr[f, 0] + yr[f, 1] + yr[f, 2]
    out[:, start : start + width] = total.astype(bf16)
    for copy in sent:
        copy.wait_send()


def scatter_kernel(gl, w_hbm, out, w, part, cs, cr, bs1, br1, bs2, br2, red, as1, ar1, as2, ar2, ys, yr,
                   csem, bsem, asem, ysem, wsem):
    pos = spot()
    loads = []
    for f, (start, width, _, _) in enumerate(CHUNKS):
        copy = pltpu.make_async_copy(w_hbm.at[pl.ds(start, width)], w.at[pl.ds(start, width)], wsem.at[f])
        copy.start()
        loads.append(copy)
    greet(pos, lines(pos, AXES))
    live = []
    for f in range(NC):
        loads[f].wait()
        g = scatter_chunk(pos, f, gl, w, part, cs, cr, bs1, br1, bs2, br2, red, as1, ar1, as2, ar2, ys, yr,
                          out, csem, bsem, asem, ysem)
        next(g)
        for other in live:
            next(other)
        live.append(g)
    run_all(live)


def scatter(gl, head):
    bf16, f32 = jnp.bfloat16, jnp.float32
    half = W // 2
    return pl.pallas_call(
        scatter_kernel,
        out_shape=jax.ShapeDtypeStruct((4, D), bf16),
        in_specs=[VM, ANY],
        out_specs=VM,
        scratch_shapes=[
            pltpu.VMEM(head.shape, bf16),
            pltpu.VMEM((NC, 16, 2, 16, W), f32),
            pltpu.VMEM((NC, 16, 16, W), bf16), pltpu.VMEM((NC, 16, 16, W), bf16),
            pltpu.VMEM((NC, 2, N, 16, half), bf16), pltpu.VMEM((NC, 2, N, 16, half), bf16),
            pltpu.VMEM((NC, 2, N, 16, W), bf16), pltpu.VMEM((NC, 2, N, 16, W), bf16),
            pltpu.VMEM((NC, N, 16, W), f32),
            pltpu.VMEM((NC, 2, 16, half), bf16), pltpu.VMEM((NC, 2, 16, half), bf16),
            pltpu.VMEM((NC, 2, 16, W), bf16), pltpu.VMEM((NC, 2, 16, W), bf16),
            pltpu.VMEM((NC, N, 4, W), f32), pltpu.VMEM((NC, 3, 4, W), f32),
            DMA((2, NC, 1)), DMA((2, NC, 4)), DMA((2, NC, 4)), DMA((2, NC, 3)), DMA((NC,)),
        ],
        compiler_params=pltpu.CompilerParams(collective_id=2, has_side_effects=True, vmem_limit_bytes=60 << 20),
        name="scatter",
    )(gl, head)


def on_device(
    hidden_states, head_weight, teacher_logits, block_lists, row_reader, tail_mass, token_weight
):
    blocks, listed_count, stored_rows, block_side = teacher_logits.shape
    slab_width = head_weight.shape[1]
    slab_blocks = slab_width // block_side
    devices = 128
    x, z, y, c = (lax.axis_index(a) for a in AXES)
    rank_self = ((x * N + z) * N + y) * 2 + c
    tokens = blocks * block_side
    owner_dev = block_lists // slab_blocks
    earlier = lax.broadcasted_iota(
        jnp.int32, (1, listed_count, listed_count), 2
    ) < lax.broadcasted_iota(jnp.int32, (1, listed_count, listed_count), 1)
    same_owner = owner_dev[:, :, None] == owner_dev[:, None, :]
    order_rank = jnp.sum((same_owner & earlier).astype(jnp.int32), axis=2)
    owned_here = owner_dev == rank_self
    within = block_lists - rank_self * slab_blocks
    place = ((row_reader // 32 * 2 + row_reader // 4 % 2) * 4 + row_reader // 8 % 4) * 4 + row_reader % 4
    token_iota = lax.broadcasted_iota(jnp.int32, (1, block_side, block_side), 1)
    token_map = (place[:, None, :] == token_iota).astype(jnp.bfloat16)
    place_iota = lax.broadcasted_iota(jnp.int32, (1, slab_blocks, 1), 1)
    target = owner_dev * MOST + order_rank
    slot_ids = lax.broadcasted_iota(jnp.int32, (1, devices * MOST, 1), 1)
    picker = (target[:, None, :] == slot_ids).astype(jnp.bfloat16)
    outgoing = jnp.einsum(
        "tsk,tkc->tsc", picker, teacher_logits[:, :, 0, :], preferred_element_type=jnp.float32
    ).astype(jnp.bfloat16)
    outgoing = outgoing.reshape(blocks, devices, MOST, block_side).transpose(1, 0, 2, 3)
    full, incoming = gather(hidden_states, outgoing.reshape(devices, blocks * MOST, block_side))
    gathered = full.reshape(tokens, D)
    logits = jnp.dot(gathered, head_weight, preferred_element_type=jnp.float32)
    incoming = incoming.reshape(devices, blocks, MOST, block_side)
    ordered = jnp.einsum(
        "tpj,jtmc->tmpc", token_map, incoming, preferred_element_type=jnp.float32
    ).astype(jnp.bfloat16)
    rank_iota = lax.broadcasted_iota(jnp.int32, (1, MOST, 1, 1), 1)
    hits = (
        owned_here[:, None, None, :]
        & (order_rank[:, None, None, :] == rank_iota)
        & (within[:, None, None, :] == place_iota[:, None, :, :])
    )
    choose = jnp.sum(hits.astype(jnp.int32), axis=3)
    teacher_slab = jnp.einsum(
        "tmb,tmpc->tpbc", choose.astype(jnp.bfloat16), ordered, preferred_element_type=jnp.float32
    )
    listed = jnp.sum(choose, axis=1)
    scores = logits.reshape(blocks, block_side, slab_blocks, block_side)
    listed_mask = (listed > 0)[:, None, :, None]
    local_smax = jnp.max(scores, axis=(2, 3))
    local_tmax = jnp.max(jnp.where(listed_mask, teacher_slab, -1e30), axis=(2, 3))
    local_sexp = jnp.exp(scores - local_smax[:, :, None, None])
    local_texp = jnp.exp(
        jnp.where(listed_mask, teacher_slab - local_tmax[:, :, None, None], -jnp.inf)
    )
    stat = jnp.stack(
        [
            jnp.concatenate([local_smax, local_tmax]),
            jnp.concatenate([jnp.sum(local_sexp, axis=(2, 3)), jnp.sum(local_texp, axis=(2, 3))]),
            jnp.concatenate(
                [
                    jnp.sum(jnp.where(listed_mask, 0.0, scores), axis=(2, 3)),
                    jnp.sum(local_texp * scores, axis=(2, 3)),
                ]
            ),
            jnp.concatenate(
                [jnp.zeros((blocks, block_side), jnp.float32), jnp.sum(local_texp * teacher_slab, axis=(2, 3))]
            ),
        ]
    )
    merged = stats_merge(stat)
    student_max, teacher_max = merged[0, :4], merged[0, 4:]
    student_sum, teacher_sum = merged[1, :4], merged[1, 4:]
    rest_total, cross_sum = merged[2, :4], merged[2, 4:]
    self_sum = merged[3, 4:]
    student_exp = jnp.exp(scores - student_max[:, :, None, None])
    teacher_exp = jnp.exp(
        jnp.where(listed_mask, teacher_slab - teacher_max[:, :, None, None], -jnp.inf)
    )

    def arranged(v):
        return v.reshape(blocks, N, N, 2, 4).transpose(0, 1, 3, 2, 4).reshape(blocks, block_side)

    tail_share = arranged(tail_mass)
    unlisted = float(devices * slab_width - block_side * listed_count)
    kept_mass = 1.0 - tail_share
    log_norm = student_max + jnp.log(student_sum)
    row_loss = (
        kept_mass * (jnp.log(kept_mass) - teacher_max - jnp.log(teacher_sum))
        + kept_mass * self_sum / teacher_sum
        + tail_share * jnp.log(tail_share / unlisted)
        - kept_mass * cross_sum / teacher_sum
        - tail_share / unlisted * rest_total
        + log_norm
    )
    token_loss = lax.dynamic_slice_in_dim(
        row_loss.reshape(tokens), x * block_side + (z * 2 + c) * 16 + y * 4, 4, 0
    )
    student_prob = student_exp / student_sum[:, :, None, None]
    teacher_prob = jnp.where(
        listed_mask,
        (kept_mass / teacher_sum)[:, :, None, None] * teacher_exp,
        (tail_share / unlisted)[:, :, None, None],
    )
    weight = arranged(token_weight)[:, :, None, None]
    grad_logits = (
        (weight * (student_prob - teacher_prob)).astype(jnp.bfloat16).reshape(tokens, slab_width)
    )
    grad_head = lax.dot_general(
        gathered, grad_logits, (((0,), (0,)), ((), ())), preferred_element_type=jnp.float32
    ).astype(jnp.bfloat16)
    grad_hidden = scatter(grad_logits, head_weight)
    return (token_loss, grad_head, grad_hidden)


def solution(mesh):
    split = Mesh(mesh.devices.reshape(N, N, N, 2), AXES)
    return jax.shard_map(
        on_device,
        mesh=split,
        in_specs=(P(AXES, None), P(None, AXES), P(None, None, AXES, None), P(), P(), P(), P()),
        out_specs=(P(AXES), P(None, AXES), P(AXES, None)),
        check_vma=False,
    )
```

time: 318 us -> 159 us (0.50)
  blocking collectives: 154 us -> 0 us
  Pallas kernels: 0 us -> 103 us
  waiting for transfers between devices: 57.8 us -> 0 us
  between operations: 14.3 us -> 0.92 us
  starting transfers between devices: 11.2 us -> 0 us
  other arithmetic: 18.2 us -> 7.71 us
  matrix products: 33 us -> 24.1 us
  local copies, waits for them, and re-layouts: 28.5 us -> 22.6 us
    unnamed x1 -> x0, blocking collectives: 116 us -> none
    pallas_call x0 -> x3, Pallas kernels: none -> 103 us  [the longest x1 47.2 us: scatter(): pl.pallas_call(scatter_kernel, out_shape=jax.ShapeDtypeStruct((4, D), bf1...]
    all_gather x1 -> x0, waiting for transfers between devices: 43.9 us -> none  [on_device(): gathered = lax.all_gather(hidden_states, VOCAB, axis=0, tiled=True)]
    all_gather x4 -> x0, blocking collectives: 37.6 us -> none  [gathered_once(): both, at, found = (lax.all_gather(jnp.concatenate(lines), axis), 0, {})]
    unnamed x21 -> x14, local copies, waits for them, and re-layouts: 23.9 us -> 2.85 us
    dot_general x0 -> x2, local copies, waits for them, and re-layouts: none -> 15.6 us  [the longest x1 13.7 us: on_device(): logits = jnp.dot(gathered, head_weight, preferred_element_type=jnp.float32)]
    all_to_all x1 -> x0, waiting for transfers between devices: 13.2 us -> none  [on_device(): lax.all_to_all(outgoing, VOCAB, split_axis=1, concat_axis=2, tiled=True)]
    dot_general x3 -> x2, matrix products: 13.1 us -> 1.87 us  [the longest x1 1.39 us: on_device(): jnp.einsum('tpj,jtmc->tmpc', token_map, incoming, preferred_element_type=...]
  transfers between devices with their start and end apart: 2 -> 0, of which waited for: 2 -> 0; matrix products, arithmetic and copies ran while one was open for 2% -> 0% of each run, Pallas kernels for 0% -> 0%
where the time goes in v1:
time: 159 us
  Pallas kernels  103 us (65%)
  matrix products  24.1 us (15%)
  local copies, waits for them, and re-layouts  22.6 us (14%)
  other arithmetic  7.71 us (5%)
    pallas_call x1, Pallas kernels, scatter(): pl.pallas_call(scatter_kernel, out_shape=jax.ShapeDtypeStruct((4, D), bf1...  47.2 us
    pallas_call x1, Pallas kernels, gather(): pl.pallas_call(gather_kernel, out_shape=(jax.ShapeDtypeStruct((N, N, 2, 1...  40.8 us
    pallas_call x1, Pallas kernels, stats_merge(): pl.pallas_call(stats_kernel, out_shape=jax.ShapeDtypeStruct(st.shape, st....  15.2 us
    dot_general x1, local copies, waits for them, and re-layouts, on_device(): logits = jnp.dot(gathered, head_weight, preferred_element_type=jnp.float32)  13.7 us
    dot_general x1, matrix products, on_device(): lax.dot_general(gathered, grad_logits, (((0,), (0,)), ((), ())), preferre...  11 us
    dot_general x1, matrix products, on_device(): logits = jnp.dot(gathered, head_weight, preferred_element_type=jnp.float32)  9.38 us

profile of v1, /device:TPU:0, one launch (start us, length us, event | category | flops | bytes accessed | tf_op | source)
XLA Modules:
  0.0 158.6 jit_solution(18249540185780338137)
XLA Ops:
  0.6 0.0 copy-start
  0.6 0.0 copy-start.5
  0.7 0.7 broadcast_compare_fusion
  1.4 0.4 convert_reduce_fusion
  1.9 0.7 broadcast_subtract_fusion.1
  2.6 0.4 convert_reduce_fusion.2
  3.0 0.0 copy-done
  3.0 0.5 fusion.15
  3.5 1.0 copy.40
  4.5 40.8 %gather.1 = (bf16[4,4,2,16,5120]{4,3,2,1,0:T(8,128)(2,1)}, bf16[128,16,128]{2,1,0:T(8,128)(2,1)}) custom-call(bf16[4,5120]{1,0:T(4,128)(2,1)} %h_ref.1, bf16[128,16,128]{2,1,0:T(8,128)(2,1)} %bitcast.143), custom_call_target="tpu_custom_call" | custom-call | tf_op jit(solution)/shard_map/gather/pallas_call | solution.py:188
  45.3 0.0 copy-done.5
  45.3 1.4 fusion.16
  46.7 0.3 copy.43
  47.0 1.8 %fusion.25 = f32[4,128,128,8]{2,3,1,0:T(8,128)} fusion(bf16[4,4,128,128]{3,1,2,0:T(4,128)(2,1)S(1)} %copy.43, s32[4,4,8]{2,1,0:T(4,128)S(1)} %get-tuple-element.13), kind=kOutput, calls=%fused_computation.52 | convolution fusion | flops 4194432 | bytes 2621952 | tf_op jit(solution)/shard_map/tmb,tmpc->tpbc/dot_general | solution.py:472
  48.8 1.9 %copy.44 = f32[4,128,128,8]{1,2,3,0:T(8,128)S(1)} copy(f32[4,128,128,8]{2,3,1,0:T(8,128)} %fusion.25) | data formatting | bytes 4194304 | tf_op jit(solution)/shard_map/tmb,tmpc->tpbc/dot_general | solution.py:472
  50.8 0.2 fusion
  51.0 13.7 %copy.50 = bf16[1024,5120]{1,0:T(8,128)(2,1)} copy(bf16[1024,5120]{0,1:T(8,128)(2,1)} %bitcast.138) | data formatting | bytes 20971520 | tf_op jit(solution)/shard_map/dot_general | solution.py:460
  64.7 9.4 %fusion.48 = (f32[4,128]{1,0:T(4,128)S(1)}, f32[4,128,8,128]{1,3,2,0:T(8,128)S(1)}) fusion(bf16[4,128,5120,1]{2,1,3,0:T(8,128)(2,1)} %bitcast.148, bf16[8,128,5120,1]{2,1,0,3:T(8,128)(2,1)} %bitcast.139), kind=kOutput, calls=%fused_computation.109 | convolution fusion | flops 5369232896 | bytes 17827840 | tf_op jit(solution)/shard_map/dot_general | solution.py:460
  74.1 0.0 copy-start.1
  74.1 0.0 copy-start.3
  74.1 0.0 copy-start.4
  74.2 1.1 fusion.4
  75.3 0.1 copy-done.1
  75.5 0.6 pad_maximum_fusion.st
  76.1 15.2 %stats_merge.1 = f32[4,8,128]{2,1,0:T(8,128)} custom-call(f32[4,8,128]{2,1,0:T(8,128)} %pad_maximum_fusion.st), custom_call_target="tpu_custom_call" | custom-call | tf_op jit(solution)/shard_map/stats_merge/pallas_call | solution.py:248
  91.3 0.0 copy-done.3
  91.3 0.1 reshape.106
  91.5 0.1 sub.120
  91.6 0.7 bitcast_divide_fusion
  92.3 0.8 slice_bitcast_fusion.1
  93.0 0.1 div.96
  93.2 0.0 copy-done.4
  93.2 0.1 reshape.112
  93.4 0.1 mul.107
  93.5 2.6 %fusion.13 = bf16[4,128,8,128]{1,3,2,0:T(8,128)(2,1)S(1)} fusion(f32[4,128,128,8]{1,2,3,0:T(8,128)S(1)} %copy.44, f32[4,128,8,128]{1,3,2,0:T(8,128)} %copy-done.1, f32[4,128]{1,0:T(4,128)S(1)} %div.96, f32[4,128]{1,0:T(4,128)S(1)} %get-tuple-element.20, f32[4,128]{1,0:T(4,128)S(1)} %bitcast_divide_fusion, f32[4,128]{1,0:T(4,128)S(1)} %get-tuple-element.19, ...), kind=kLoop, calls=%fused_computation.18 | loop fusion | flops 4718592 | bytes 5255200 | tf_op jit(solution)/shard_map/convert_element_type | solution.py:535
  96.1 0.7 copy.46
  96.8 11.0 %convolution_convert_fusion = bf16[5120,1024]{1,0:T(8,128)(2,1)} fusion(bf16[512,5120]{1,0:T(8,128)(2,1)} %bitcast.149, bf16[64,8,8,128]{3,2,1,0:T(8,128)(2,1)S(1)} %bitcast.141), kind=kOutput, calls=%fused_computation | convolution fusion | flops 5373952000 | bytes 16777216 | tf_op jit(solution)/shard_map/dot_general | solution.py:537
  107.9 1.3 copy.61
  109.1 0.0 copy-start.2
  109.1 47.2 %scatter.1 = bf16[4,5120]{1,0:T(4,128)(2,1)} custom-call(bf16[512,1024]{1,0:T(8,128)(2,1)} %bitcast.140, bf16[5120,1024]{1,0:T(8,128)(2,1)} %w_hbm.1), custom_call_target="tpu_custom_call" | custom-call | tf_op jit(solution)/shard_map/scatter/pallas_call | solution.py:407
  156.4 0.1 reshape.107
  156.5 0.0 copy-done.2
  156.6 0.6 dynamic_slice.3
  157.2 1.4 copy.64
  (12 shorter events, 0.2 us)
Async XLA Ops:
  0.6 2.4 %copy-start = (bf16[4,256,1,128]{3,1,2,0:T(8,128)(2,1)S(1)}, bf16[4,256,1,128]{3,1,2,0:T(8,128)(2,1)}, u32[]{:S(2)}) copy-start(bf16[4,256,1,128]{3,1,2,0:T(8,128)(2,1)} %param.9) | copy-start | bytes 786436
  0.6 44.6 %copy-start.5 = (s32[4,128]{1,0:T(4,128)S(1)}, s32[4,128]{1,0:T(4,128)}, u32[]{:S(2)}) copy-start(s32[4,128]{1,0:T(4,128)} %param.11) | copy-start | bytes 6148
  74.1 1.3 copy-start.1
  74.1 17.2 %copy-start.3 = (f32[512]{0:T(512)S(1)}, f32[512]{0:T(512)}, u32[]{:S(2)}) copy-start(f32[512]{0:T(512)} %param.12) | copy-start | bytes 6148
  74.1 19.0 %copy-start.4 = (f32[512]{0:T(512)S(1)}, f32[512]{0:T(512)}, u32[]{:S(2)}) copy-start(f32[512]{0:T(512)} %param.13) | copy-start | bytes 6148
  109.1 47.4 %copy-start.2 = (f32[4,8,128]{2,1,0:T(8,128)S(1)}, f32[4,8,128]{2,1,0:T(8,128)}, u32[]{:S(2)}) copy-start(f32[4,8,128]{2,1,0:T(8,128)} %stats_merge.1) | copy-start | bytes 49156

commit v2 on v1

v2 whole, which is shorter than its diff:
```python
import functools

import jax
import jax.numpy as jnp
from jax import lax
from jax.experimental import pallas as pl
from jax.experimental.pallas import tpu as pltpu
from jax.sharding import Mesh
from jax.sharding import PartitionSpec as P

MOST = 4
AXES = ("x", "z", "y", "c")
N = 4
D = 5120
CHUNKS = ((0, 1280, "x", "z"), (1280, 1280, "z", "x"), (2560, 1280, "x", "z"), (3840, 1280, "z", "x"))
NC = len(CHUNKS)
DMA = pltpu.SemaphoreType.DMA
REGULAR = pltpu.SemaphoreType.REGULAR
VM = pl.BlockSpec(memory_space=pltpu.VMEM)
ANY = pl.BlockSpec(memory_space=pl.ANY)


def spot():
    return {a: lax.axis_index(a) for a in AXES}


def moved(pos, axis, step):
    if axis == "c":
        return {"c": 1 - pos["c"]}
    return {axis: lax.rem(pos[axis] + step + N, N)}


def remote(src, dst, send, recv, device):
    return pltpu.make_async_remote_copy(
        src_ref=src, dst_ref=dst, send_sem=send, recv_sem=recv,
        device_id=device, device_id_type=pl.DeviceIdType.MESH,
    )


def greet(pos, partners):
    barrier = pltpu.get_barrier_semaphore()
    for device in partners:
        pl.semaphore_signal(barrier, inc=1, device_id=device, device_id_type=pl.DeviceIdType.MESH)
    pl.semaphore_wait(barrier, len(partners))


def lines(pos, axes):
    return [moved(pos, a, s) for a in axes for s in ((1,) if a == "c" else (1, 2, 3))]


def gather_chunk(pos, f, full, asend, arecv, bsend, brecv, csend, crecv):
    start, width, A, B = CHUNKS[f]
    half = width // 2
    a, b, c = pos[A], pos[B], pos["c"]
    every, low, high = pl.ds(start, width), pl.ds(start, half), pl.ds(start + half, half)
    sent = []

    def unit(off_a, off_b, cols):
        at = {A: lax.rem(a + off_a + N, N), B: lax.rem(b + off_b + N, N)}
        return full.at[at["x"], at["z"], c, :, cols]

    def send(ref, send_sem, recv_sem, axis, step):
        copy = remote(ref, ref, send_sem, recv_sem, moved(pos, axis, step))
        copy.start()
        sent.append(copy)

    def arrived(ref, recv_sem):
        remote(ref, ref, recv_sem, recv_sem, moved(pos, "c", 1)).wait_recv()

    offs = (0, -1, 1, 2)

    def onward(j):
        ref = unit(offs[j], 0, every)
        send(ref, bsend.at[f, j, 0], brecv.at[f, j, 0], B, 1)
        send(ref, bsend.at[f, j, 1], brecv.at[f, j, 1], B, -1)
        across(j, 0)

    def across(j, k):
        send(unit(offs[j], offs[k], every), csend.at[f, j, k], crecv.at[f, j, k], "c", 1)

    ref = unit(0, 0, every)
    send(ref, asend.at[f, 0], arecv.at[f, 0], A, 1)
    send(ref, asend.at[f, 1], arecv.at[f, 1], A, -1)
    onward(0)
    yield
    arrived(unit(-1, 0, every), arecv.at[f, 0])
    send(unit(-1, 0, low), asend.at[f, 2], arecv.at[f, 2], A, 1)
    onward(1)
    arrived(unit(1, 0, every), arecv.at[f, 1])
    send(unit(1, 0, high), asend.at[f, 3], arecv.at[f, 3], A, -1)
    onward(2)
    yield

    def relay(j):
        arrived(unit(offs[j], -1, every), brecv.at[f, j, 0])
        send(unit(offs[j], -1, low), bsend.at[f, j, 2], brecv.at[f, j, 2], B, 1)
        across(j, 1)
        arrived(unit(offs[j], 1, every), brecv.at[f, j, 1])
        send(unit(offs[j], 1, high), bsend.at[f, j, 3], brecv.at[f, j, 3], B, -1)
        across(j, 2)

    relay(0)
    yield
    arrived(unit(2, 0, low), arecv.at[f, 2])
    arrived(unit(2, 0, high), arecv.at[f, 3])
    onward(3)
    yield
    relay(1)
    relay(2)
    yield
    relay(3)
    yield
    for j in range(4):
        arrived(unit(offs[j], 2, low), brecv.at[f, j, 2])
        arrived(unit(offs[j], 2, high), brecv.at[f, j, 3])
        across(j, 3)
    yield
    for j in range(4):
        for k in range(4):
            at = {A: lax.rem(a + offs[j] + N, N), B: lax.rem(b + offs[k] + N, N)}
            arrived(full.at[at["x"], at["z"], 1 - c, :, every], crecv.at[f, j, k])
    for copy in sent:
        copy.wait_send()


def run_all(gens):
    gens = list(gens)
    while gens:
        for g in list(gens):
            try:
                next(g)
            except StopIteration:
                gens.remove(g)


def plane_line(pos):
    x, z, y, c = (pos[a] for a in AXES)
    plane = [{"z": lax.rem(z + dz, N), "y": lax.rem(y + dy, N)} for dz in range(N) for dy in range(N) if dz or dy]
    line = [{"x": lax.rem(x + dx, N), "c": lax.rem(c + dc, 2)} for dx in range(N) for dc in range(2) if dx or dc]
    return plane, line


W = CHUNKS[0][1]
TILE = 256
PIECE = 512


def scatter_chunk(pos, f, gl, w, part, cs, cr, bs1, br1, bs2, br2, red, as1, ar1, ys, yr, out, csem, bsem, asem, ysem):
    start, width, A, B = CHUNKS[f]
    half = width // 2
    a, b, c, y = pos[A], pos[B], pos["c"], pos["y"]
    f32, bf16 = jnp.float32, jnp.bfloat16
    sent = []

    def index(ia, ib):
        at = {A: ia, B: ib}
        return at["x"] * N + at["z"]

    def shift(p, s):
        return lax.rem(p + s + N, N)

    def send(src, dst, sems, k, axis, step):
        copy = remote(src, dst, sems.at[0, f, k], sems.at[1, f, k], moved(pos, axis, step))
        copy.start()
        sent.append(copy)

    def arrived(ref, sems, k):
        remote(ref, ref, sems.at[0, f, k], sems.at[1, f, k], moved(pos, "c", 1)).wait_recv()

    def product(i, carry):
        rows = w[pl.ds(pl.multiple_of(start + i * TILE, TILE), TILE), :]
        got = lax.dot_general(gl[...], rows, (((1,), (1,)), ((), ())), preferred_element_type=f32)
        part[f, :, :, :, pl.ds(pl.multiple_of(i * TILE, TILE), TILE)] = got.reshape(16, 2, 16, TILE)
        return carry

    lax.fori_loop(0, width // TILE, product, 0)

    def other(u, carry):
        cs[f, u] = part[f, u, 1 - c].astype(bf16)
        return carry

    lax.fori_loop(0, 16, other, 0)
    send(cs.at[f], cr.at[f], csem, 0, "c", 1)
    yield
    arrived(cr.at[f], csem, 0)

    def chip(u):
        return part[f, u, c] + cr[f, u].astype(f32)

    def opposite(i, carry):
        v = chip(index(i, shift(b, 2))).astype(bf16)
        bs1[f, 0, i] = v[:, :half]
        bs1[f, 1, i] = v[:, half:]
        return carry

    lax.fori_loop(0, N, opposite, 0)
    send(bs1.at[f, 0], br1.at[f, 0], bsem, 0, B, 1)
    send(bs1.at[f, 1], br1.at[f, 1], bsem, 1, B, -1)
    yield
    arrived(br1.at[f, 0], bsem, 0)

    def up(i, carry):
        v = chip(index(i, shift(b, 1)))
        bs2[f, 0, i, :, :half] = (v[:, :half] + br1[f, 0, i].astype(f32)).astype(bf16)
        bs2[f, 0, i, :, half:] = v[:, half:].astype(bf16)
        return carry

    lax.fori_loop(0, N, up, 0)
    send(bs2.at[f, 0], br2.at[f, 0], bsem, 2, B, 1)
    arrived(br1.at[f, 1], bsem, 1)

    def down(i, carry):
        v = chip(index(i, shift(b, -1)))
        bs2[f, 1, i, :, :half] = v[:, :half].astype(bf16)
        bs2[f, 1, i, :, half:] = (v[:, half:] + br1[f, 1, i].astype(f32)).astype(bf16)
        return carry

    lax.fori_loop(0, N, down, 0)
    send(bs2.at[f, 1], br2.at[f, 1], bsem, 3, B, -1)
    yield
    arrived(br2.at[f, 0], bsem, 2)
    arrived(br2.at[f, 1], bsem, 3)

    def kept(i, carry):
        red[f, i] = chip(index(i, b)) + br2[f, 0, i].astype(f32) + br2[f, 1, i].astype(f32)
        return carry

    lax.fori_loop(0, N, kept, 0)
    for d in (2, 1, 3):
        as1[f, d - 1] = red[f, shift(a, d)].astype(bf16)
        send(as1.at[f, d - 1], ar1.at[f, d - 1], asem, d - 1, A, d)
    yield
    for d in (1, 2, 3):
        arrived(ar1.at[f, d - 1], asem, d - 1)
    v = red[f, a] + ar1[f, 0].astype(f32) + ar1[f, 1].astype(f32) + ar1[f, 2].astype(f32)
    for k in range(N):
        ys[f, k] = v[4 * k : 4 * k + 4, :]
    for d in (2, 1, 3):
        send(ys.at[f, shift(y, d)], yr.at[f, d - 1], ysem, d - 1, "y", d)
    yield
    for d in (1, 2, 3):
        arrived(yr.at[f, d - 1], ysem, d - 1)
    total = ys[f, y] + yr[f, 0] + yr[f, 1] + yr[f, 2]
    out[:, start : start + width] = total.astype(bf16)
    for copy in sent:
        copy.wait_send()


def step_kernel(h, tout, tmap, tcon, extra, choose, listed, w_hbm, loss, gx, gh,
                full, inc, rows, wide, w, L, gl, T32, TV, msg, near, mid, far, lmsg, lnear, lmid, lfar,
                part, cs, cr, bs1, br1, bs2, br2, red, as1, ar1, ys, yr, stage,
                wsem, ysend, yrecv, asend, arecv, bsend, brecv, csend, crecv, tsend, trecv, own, every,
                xsem, csem, bsem, asem, rsem, gsem):
    f32, bf16 = jnp.float32, jnp.bfloat16
    pos = spot()
    x, z, y, c = (pos[a] for a in AXES)
    me = ((x * N + z) * N + y) * 2 + c
    plane, line = plane_line(pos)
    loads = []
    for f, (start, width, _, _) in enumerate(CHUNKS):
        copy = pltpu.make_async_copy(w_hbm.at[pl.ds(start, width)], w.at[pl.ds(start, width)], wsem.at[f])
        copy.start()
        loads.append(copy)
    greet(pos, plane + line)

    first = []
    for d in (2, 1, 3):
        copy = remote(h, rows.at[y], ysend.at[d - 1], yrecv.at[d - 1], moved(pos, "y", d))
        copy.start()
        first.append(copy)
    mine = pltpu.make_async_copy(h, rows.at[y], own.at[0])
    mine.start()
    keep = pltpu.make_async_copy(tout.at[me], inc.at[me], own.at[1])
    keep.start()
    for device in line:
        pl.semaphore_signal(every, inc=1, device_id=device, device_id_type=pl.DeviceIdType.MESH)
    mine.wait()
    for d in (1, 2, 3):
        ref = rows.at[lax.rem(y - d + N, N)]
        remote(ref, ref, ysend.at[d - 1], yrecv.at[d - 1], moved(pos, "y", d)).wait_recv()
    for k in range(N):
        wide[4 * k : 4 * k + 4, :] = rows[k].astype(f32)
    full[x, z, c] = wide[...].astype(bf16)
    gens = [gather_chunk(pos, f, full, asend, arecv, bsend, brecv, csend, crecv) for f in range(NC)]
    for g in gens:
        next(g)
    pl.semaphore_wait(every, len(line))

    def one(k, carry):
        to = lax.rem(me + k, 128)
        device = {"x": to // 32, "z": lax.rem(to // 8, N), "y": lax.rem(to // 2, N), "c": lax.rem(to, 2)}
        remote(tout.at[to], inc.at[me], tsend, trecv, device).start()
        return carry

    lax.fori_loop(1, 128, one, 0)

    def logits_part(f, lo, hi):
        start, width = CHUNKS[f][:2]

        def tile(i, carry):
            cols = pl.ds(pl.multiple_of(i * TILE, TILE), TILE)
            got = jnp.dot(
                full[:, :, :, :, start : start + width].reshape(512, width),
                w[start : start + width, cols],
                preferred_element_type=f32,
            )
            if f == 0:
                L[:, cols] = got
            else:
                L[:, cols] += got
            return carry

        lax.fori_loop(lo, hi, tile, 0)

    def finish(g):
        for _ in g:
            pass

    g0, g1, g2, g3 = gens
    for _ in range(3):
        next(g0), next(g1)
    next(g2), next(g3)
    for _ in range(2):
        next(g0), next(g1)
        next(g2), next(g3)
    finish(g0)
    next(g2), next(g3)
    loads[0].wait()
    logits_part(0, 0, 2)
    next(g2), next(g3)
    logits_part(0, 2, 4)
    next(g2), next(g3)
    finish(g1)
    loads[1].wait()
    logits_part(1, 0, 4)
    finish(g2)
    loads[2].wait()
    logits_part(2, 0, 4)
    finish(g3)
    loads[3].wait()
    logits_part(3, 0, 4)
    for copy in first:
        copy.wait_send()

    for t in range(N):
        r = slice(128 * t, 128 * t + 128)
        top = L[r, :128]
        for b in range(1, 8):
            top = jnp.maximum(top, L[r, 128 * b : 128 * b + 128])
        col = jnp.max(top, axis=1, keepdims=True)
        acc = jnp.exp(L[r, :128] - col)
        for b in range(1, 8):
            acc = acc + jnp.exp(L[r, 128 * b : 128 * b + 128] - col)
        msg[0, t : t + 1] = jnp.max(top.T, axis=0, keepdims=True)
        msg[1, t : t + 1] = jnp.sum(acc.T, axis=0, keepdims=True)
    msg[0, 4:8] = tcon[0:4]
    msg[1, 4:8] = jnp.zeros((4, 128), f32)

    def merge(parts):
        top = parts[0][0]
        for p in parts[1:]:
            top = jnp.maximum(top, p[0])
        total = 0.0
        for p in parts:
            total += p[1] * jnp.exp(p[0] - top)
        return top, total

    for device in plane:
        remote(msg, near.at[z * N + y], xsem.at[0], xsem.at[1], device).start()
    near[z * N + y] = msg[...]

    part_inc = inc.at[pl.ds(0, 127)]
    remote(part_inc, part_inc, tsend, trecv, moved(pos, "c", 1)).wait()
    keep.wait()
    T32[...] = inc[...].reshape(2048, 128).astype(f32)

    def teacher(t):
        stored = jnp.concatenate(
            [T32[pl.ds(t * MOST + m, 128, stride=16), :] for m in range(MOST)], axis=1
        ).astype(bf16)
        ordered = jnp.dot(tmap[t], stored, preferred_element_type=f32)
        for b in range(8):
            v = choose[t * 32 + b] * ordered[:, :128]
            for m in range(1, MOST):
                v = v + choose[t * 32 + m * 8 + b] * ordered[:, 128 * m : 128 * m + 128]
            TV[t, b] = v.astype(bf16)

    teacher(0)
    teacher(1)
    group = near.at[pl.ds(0, 15)]
    remote(group, group, xsem.at[0], xsem.at[1], plane[0]).wait()
    mid[0], mid[1] = merge([near[i] for i in range(16)])
    for device in line:
        remote(mid, far.at[x * 2 + c], xsem.at[2], xsem.at[3], device).start()
    far[x * 2 + c] = mid[...]
    teacher(2)
    teacher(3)
    group = far.at[pl.ds(0, 7)]
    remote(group, group, xsem.at[2], xsem.at[3], line[0]).wait()
    top, total = merge([far[i] for i in range(8)])

    log_norm = top[0:4] + jnp.log(total[0:4])
    tail = extra[0:4]
    weight = extra[4:8]
    kept = jnp.log(1.0 - tail) - top[4:8]
    tail_prob = tail / UNLISTED
    tail_log = jnp.log(tail_prob)

    def column(v, t):
        return jnp.broadcast_to(v[t : t + 1], (128, 128)).T

    lmsg[...] = jnp.zeros((8, 128), f32)
    for t in range(N):
        r = slice(128 * t, 128 * t + 128)
        norm_c, weight_c, kept_c = column(log_norm, t), column(weight, t), column(kept, t)
        prob_c, log_c = column(tail_prob, t), column(tail_log, t)
        acc = jnp.zeros((128, 128), f32)
        for b in range(8):
            scores = L[r, 128 * b : 128 * b + 128]
            on = listed[t * 8 + b]
            off = 1.0 - on
            listed_log = TV[t, b].astype(f32) + kept_c
            q = on * jnp.exp(listed_log) + off * prob_c
            log_q = on * listed_log + off * log_c
            gap = scores - norm_c
            gl[r, 128 * b : 128 * b + 128] = (weight_c * (jnp.exp(gap) - q)).astype(bf16)
            acc = acc + q * (log_q - gap)
        lmsg[t : t + 1] = jnp.sum(acc.T, axis=0, keepdims=True)

    stores = [None, None]
    count = [0]

    def head_piece():
        i = count[0]
        if i == D // PIECE:
            return
        count[0] = i + 1
        slot = i % 2
        if stores[slot] is not None:
            stores[slot].wait()
        cols = slice(i * PIECE, i * PIECE + PIECE)

        def tile(n, carry):
            some = pl.ds(pl.multiple_of(n * TILE, TILE), TILE)
            got = lax.dot_general(
                full[:, :, :, :, cols].reshape(512, PIECE), gl[:, some], (((0,), (0,)), ((), ())),
                preferred_element_type=f32,
            )
            stage[slot, :, some] = got.astype(bf16)
            return carry

        lax.fori_loop(0, 1024 // TILE, tile, 0)
        stores[slot] = pltpu.make_async_copy(stage.at[slot], gh.at[pl.ds(i * PIECE, PIECE)], gsem.at[slot])
        stores[slot].start()

    s0, s1, s2, s3 = [
        scatter_chunk(pos, f, gl, w, part, cs, cr, bs1, br1, bs2, br2, red, as1, ar1, ys, yr, gx, csem, bsem, asem, rsem)
        for f in range(NC)
    ]
    next(s0)
    next(s1)
    next(s0)
    next(s2)
    next(s1)
    next(s3)
    next(s0)
    next(s2)
    next(s1)
    next(s3)
    for device in plane:
        remote(lmsg, lnear.at[z * N + y], xsem.at[4], xsem.at[5], device).start()
    lnear[z * N + y] = lmsg[...]
    head_piece()
    head_piece()
    next(s0)
    next(s1)
    head_piece()
    next(s2)
    next(s3)
    group = lnear.at[pl.ds(0, 15)]
    remote(group, group, xsem.at[4], xsem.at[5], plane[0]).wait()
    total = lnear[0]
    for i in range(1, 16):
        total = total + lnear[i]
    lmid[...] = total
    for device in line:
        remote(lmid, lfar.at[x * 2 + c], xsem.at[6], xsem.at[7], device).start()
    lfar[x * 2 + c] = lmid[...]
    head_piece()
    next(s0)
    next(s1)
    head_piece()
    head_piece()
    next(s2)
    next(s3)
    head_piece()
    finish(s0)
    finish(s1)
    head_piece()
    next(s2)
    next(s3)
    head_piece()
    head_piece()
    group = lfar.at[pl.ds(0, 7)]
    remote(group, group, xsem.at[6], xsem.at[7], line[0]).wait()
    total = lfar[0]
    for i in range(1, 8):
        total = total + lfar[i]
    loss[...] = total
    finish(s2)
    finish(s3)
    for copy in stores:
        copy.wait()


UNLISTED = 98304.0


def step(hidden, outgoing, token_map, own_norm, extra, choose, listed, head):
    bf16, f32 = jnp.bfloat16, jnp.float32
    half = W // 2
    V = pltpu.VMEM
    SM = pl.BlockSpec(memory_space=pltpu.SMEM)
    return pl.pallas_call(
        step_kernel,
        out_shape=(
            jax.ShapeDtypeStruct((8, 128), f32),
            jax.ShapeDtypeStruct((4, D), bf16),
            jax.ShapeDtypeStruct(head.shape, bf16),
        ),
        in_specs=[VM, VM, VM, VM, VM, SM, SM, ANY],
        out_specs=(VM, VM, ANY),
        scratch_shapes=[
            V((N, N, 2, 16, D), bf16),
            V((128, 16, 128), bf16),
            V((N, 4, D), bf16),
            V((16, D), f32),
            V(head.shape, bf16),
            V((512, 1024), f32),
            V((512, 1024), bf16),
            V((2048, 128), f32),
            V((N, 8, 128, 128), bf16),
            V((2, 8, 128), f32), V((16, 2, 8, 128), f32), V((2, 8, 128), f32), V((8, 2, 8, 128), f32),
            V((8, 128), f32), V((16, 8, 128), f32), V((8, 128), f32), V((8, 8, 128), f32),
            V((NC, 16, 2, 16, W), f32),
            V((NC, 16, 16, W), bf16), V((NC, 16, 16, W), bf16),
            V((NC, 2, N, 16, half), bf16), V((NC, 2, N, 16, half), bf16),
            V((NC, 2, N, 16, W), bf16), V((NC, 2, N, 16, W), bf16),
            V((NC, N, 16, W), f32),
            V((NC, 3, 16, W), bf16), V((NC, 3, 16, W), bf16),
            V((NC, N, 4, W), f32), V((NC, 3, 4, W), f32),
            V((2, PIECE, 1024), bf16),
            DMA((NC,)),
            DMA((3,)), DMA((3,)),
            DMA((NC, 4)), DMA((NC, 4)),
            DMA((NC, 4, 4)), DMA((NC, 4, 4)),
            DMA((NC, 4, 4)), DMA((NC, 4, 4)),
            DMA, DMA, DMA((2,)), REGULAR,
            DMA((8,)),
            DMA((2, NC, 1)), DMA((2, NC, 4)), DMA((2, NC, 3)), DMA((2, NC, 3)), DMA((2,)),
        ],
        compiler_params=pltpu.CompilerParams(collective_id=0, has_side_effects=True, vmem_limit_bytes=67043328),
        name="step",
    )(hidden, outgoing, token_map, own_norm, extra, choose, listed, head)


def on_device(
    hidden_states, head_weight, teacher_logits, block_lists, row_reader, tail_mass, token_weight
):
    blocks, listed_count, stored_rows, block_side = teacher_logits.shape
    slab_width = head_weight.shape[1]
    slab_blocks = slab_width // block_side
    devices = 128
    x, z, y, c = (lax.axis_index(a) for a in AXES)
    rank_self = ((x * N + z) * N + y) * 2 + c
    owner_dev = block_lists // slab_blocks
    earlier = lax.broadcasted_iota(
        jnp.int32, (1, listed_count, listed_count), 2
    ) < lax.broadcasted_iota(jnp.int32, (1, listed_count, listed_count), 1)
    same_owner = owner_dev[:, :, None] == owner_dev[:, None, :]
    order_rank = jnp.sum((same_owner & earlier).astype(jnp.int32), axis=2)
    owned_here = owner_dev == rank_self
    within = block_lists - rank_self * slab_blocks
    place = ((row_reader // 32 * 2 + row_reader // 4 % 2) * 4 + row_reader // 8 % 4) * 4 + row_reader % 4
    token_iota = lax.broadcasted_iota(jnp.int32, (1, block_side, block_side), 1)
    token_map = (place[:, None, :] == token_iota).astype(jnp.bfloat16)
    place_iota = lax.broadcasted_iota(jnp.int32, (1, slab_blocks, 1), 1)
    target = owner_dev * MOST + order_rank
    slot_ids = lax.broadcasted_iota(jnp.int32, (1, devices * MOST, 1), 1)
    picker = (target[:, None, :] == slot_ids).astype(jnp.bfloat16)
    outgoing = jnp.einsum(
        "tsk,tkc->tsc", picker, teacher_logits[:, :, 0, :], preferred_element_type=jnp.float32
    ).astype(jnp.bfloat16)
    outgoing = outgoing.reshape(blocks, devices, MOST, block_side).transpose(1, 0, 2, 3)
    outgoing = outgoing.reshape(devices, blocks * MOST, block_side)
    rank_iota = lax.broadcasted_iota(jnp.int32, (1, MOST, 1, 1), 1)
    hits = (
        owned_here[:, None, None, :]
        & (order_rank[:, None, None, :] == rank_iota)
        & (within[:, None, None, :] == place_iota[:, None, :, :])
    )
    choose = jnp.sum(hits.astype(jnp.float32), axis=3)
    listed = jnp.sum(choose, axis=1)
    stored = teacher_logits[:, :, 0, :].astype(jnp.float32)
    stored_max = jnp.max(stored, axis=(1, 2))
    stored_norm = stored_max + jnp.log(jnp.sum(jnp.exp(stored - stored_max[:, None, None]), axis=(1, 2)))
    lane = lax.broadcasted_iota(jnp.int32, (blocks, block_side), 1)
    mine = lax.dynamic_slice_in_dim(place, rank_self, 1, 1)
    own_norm = jnp.where(lane == mine, stored_norm[:, None], -1e30)

    def arranged(v):
        return v.reshape(blocks, N, N, 2, 4).transpose(0, 1, 3, 2, 4).reshape(blocks, block_side)

    extra = jnp.concatenate([arranged(tail_mass), arranged(token_weight)])
    row_loss, grad_hidden, grad_head = step(
        hidden_states, outgoing, token_map, own_norm, extra, choose.reshape(-1), listed.reshape(-1), head_weight
    )
    token_loss = lax.dynamic_slice(row_loss, (x, (z * 2 + c) * 16 + y * 4), (1, 4)).reshape(4)
    return (token_loss, grad_head, grad_hidden)


def solution(mesh):
    split = Mesh(mesh.devices.reshape(N, N, N, 2), AXES)
    return jax.shard_map(
        on_device,
        mesh=split,
        in_specs=(P(AXES, None), P(None, AXES), P(None, None, AXES, None), P(), P(), P(), P()),
        out_specs=(P(AXES), P(None, AXES), P(AXES, None)),
        check_vma=False,
    )
```

time: 159 us -> 120 us (0.75)
  matrix products: 24.1 us -> 1.43 us
  Pallas kernels: 103 us -> 95.5 us
  local copies, waits for them, and re-layouts: 22.6 us -> 15.5 us
    dot_general x4 -> x0, matrix products: 23.6 us -> none  [the longest x1 11 us: on_device(): lax.dot_general(gathered, grad_logits, (((0,), (0,)), ((), ())), preferre...]
    dot_general x2 -> x0, local copies, waits for them, and re-layouts: 15.6 us -> none  [the longest x1 13.7 us: on_device(): logits = jnp.dot(gathered, head_weight, preferred_element_type=jnp.float32)]
    pallas_call x3 -> x1, Pallas kernels: 103 us -> 95.5 us  [step(): pl.pallas_call(step_kernel, out_shape=(jax.ShapeDtypeStruct((8, 128), f32...]
    unnamed x14 -> x4, local copies, waits for them, and re-layouts: 2.85 us -> 9.94 us
    reshape x0 -> x3, local copies, waits for them, and re-layouts: none -> 2.49 us  [the longest x1 1.26 us: on_device(): lax.dynamic_slice(row_loss, (x, (z * 2 + c) * 16 + y * 4), (1, 4))]
    convert_element_type x1, other arithmetic: 2.62 us -> 0.68 us  [on_device(): token_map = (place[:, None, :] == token_iota).astype(jnp.bfloat16)]
where the time goes in v2:
time: 120 us
  Pallas kernels  95.5 us (80%)
  local copies, waits for them, and re-layouts  15.5 us (13%)
  other arithmetic  6.88 us (6%)
  matrix products  1.43 us (1%)
    pallas_call x1, Pallas kernels, step(): pl.pallas_call(step_kernel, out_shape=(jax.ShapeDtypeStruct((8, 128), f32...  95.5 us
    unnamed x4, local copies, waits for them, and re-layouts  9.94 us

profile of v2, /device:TPU:0, one launch (start us, length us, event | category | flops | bytes accessed | tf_op | source)
XLA Modules:
  0.0 120.1 jit_solution(17783233490234790327)
XLA Ops:
  0.6 1.1 reduce_max.14
  1.8 1.2 %exponential_reduce_fusion = f32[4]{0:T(128)S(1)} fusion(bf16[4,256,1,128]{3,1,2,0:T(8,128)(2,1)} %param.9, f32[4]{0:T(128)S(1)} %reduce_max.15), kind=kLoop, calls=%fused_computation.5 | loop fusion | flops 393212 | bytes 262176 | tf_op jit(solution)/shard_map/reduce_sum | solution.py:606
  3.0 0.7 fusion.14
  3.7 0.2 dynamic-slice_reduce_fusion
  3.9 0.6 fusion.18.tcon
  4.5 0.7 broadcast_subtract_fusion
  5.2 0.7 broadcast_compare_fusion
  5.9 0.8 reshape.78
  6.7 0.1 reshape.79
  6.9 0.8 reshape.80
  7.7 0.1 reshape.81
  7.8 0.6 pad_maximum_fusion.extra
  8.5 0.4 convert_reduce_fusion
  8.9 0.1 convert_reduce_fusion.1
  9.0 0.6 reshape.83.listed
  9.6 0.6 reshape.82.choose
  10.2 0.7 fusion.4.tmap
  10.9 1.4 %fusion.1 = bf16[4,512,128]{2,1,0:T(8,128)(2,1)S(1)} fusion(s32[4,256]{1,0:T(4,128)S(1)} %multiply_add_fusion, bf16[4,256,1,128]{3,1,2,0:T(8,128)(2,1)} %param.9), kind=kOutput, calls=%fused_computation.2 | convolution fusion | flops 135004160 | bytes 790528 | tf_op jit(solution)/shard_map/tsk,tkc->tsc/dot_general | solution.py:591
  12.4 1.0 copy.14
  13.3 95.5 %step.1 = (f32[8,128]{1,0:T(8,128)}, bf16[4,5120]{1,0:T(4,128)(2,1)}, bf16[5120,1024]{1,0:T(8,128)(2,1)}) custom-call(bf16[4,5120]{1,0:T(4,128)(2,1)} %h.1, bf16[128,16,128]{2,1,0:T(8,128)(2,1)} %bitcast.12, bf16[4,128,128]{2,1,0:T(8,128)(2,1)} %fusion.4.tmap, f32[4,128]{1,0:T(4,128)} %fusion.18.tcon, f32[8,128]{1,0:T(8,128)} %pad_maximum_fusion.extra, ...), custom_call_target="tpu_custom_call" | custom-call | tf_op jit(solution)/shard_map/step/pallas_call | solution.py:524
  108.9 1.3 %dynamic-slice_bitcast_fusion = f32[4]{0:T(128)} fusion(f32[8,128]{1,0:T(8,128)} %get-tuple-element.6, s32[]{:T(128)S(6)} %select_n.53, s32[]{:T(128)S(6)} %select_n.54), kind=kLoop, calls=%fused_computation.58 | loop fusion | bytes 40 | tf_op jit(solution)/shard_map/reshape | solution.py:618
  110.1 0.0 copy-start
  110.1 9.3 %copy.19 = bf16[5120,1024]{1,0:T(8,128)(2,1)} copy(bf16[5120,1024]{1,0:T(8,128)(2,1)} %get-tuple-element.17) | data formatting | bytes 20971520
  119.4 0.0 copy-done
  119.4 0.6 copy.20
  (8 shorter events, 0.1 us)
Async XLA Ops:
  110.1 9.3 %copy-start = (bf16[4,5120]{1,0:T(4,128)(2,1)S(1)}, bf16[4,5120]{1,0:T(4,128)(2,1)}, u32[]{:S(2)}) copy-start(bf16[4,5120]{1,0:T(4,128)(2,1)} %get-tuple-element.18) | copy-start | bytes 122884

commit v3 on v2

v3 whole, which is shorter than its diff:
```python
import functools

import jax
import jax.numpy as jnp
from jax import lax
from jax.experimental import pallas as pl
from jax.experimental.pallas import tpu as pltpu
from jax.sharding import Mesh
from jax.sharding import PartitionSpec as P

MOST = 4
AXES = ("x", "z", "y", "c")
N = 4
D = 5120
CHUNKS = ((0, 1280, "x", "z"), (1280, 1280, "z", "x"), (2560, 1280, "x", "z"), (3840, 1280, "z", "x"))
NC = len(CHUNKS)
DMA = pltpu.SemaphoreType.DMA
REGULAR = pltpu.SemaphoreType.REGULAR
VM = pl.BlockSpec(memory_space=pltpu.VMEM)
ANY = pl.BlockSpec(memory_space=pl.ANY)


def spot():
    return {a: lax.axis_index(a) for a in AXES}


def moved(pos, axis, step):
    if axis == "c":
        return {"c": 1 - pos["c"]}
    return {axis: lax.rem(pos[axis] + step + N, N)}


def remote(src, dst, send, recv, device):
    return pltpu.make_async_remote_copy(
        src_ref=src, dst_ref=dst, send_sem=send, recv_sem=recv,
        device_id=device, device_id_type=pl.DeviceIdType.MESH,
    )


def greet(pos, partners):
    barrier = pltpu.get_barrier_semaphore()
    for device in partners:
        pl.semaphore_signal(barrier, inc=1, device_id=device, device_id_type=pl.DeviceIdType.MESH)
    pl.semaphore_wait(barrier, len(partners))


def lines(pos, axes):
    return [moved(pos, a, s) for a in axes for s in ((1,) if a == "c" else (1, 2, 3))]


def gather_chunk(pos, f, full, asend, arecv, bsend, brecv, csend, crecv):
    start, width, A, B = CHUNKS[f]
    half = width // 2
    a, b, c = pos[A], pos[B], pos["c"]
    every, low, high = pl.ds(start, width), pl.ds(start, half), pl.ds(start + half, half)
    sent = []

    def unit(off_a, off_b, cols):
        at = {A: lax.rem(a + off_a + N, N), B: lax.rem(b + off_b + N, N)}
        return full.at[at["x"], at["z"], c, :, cols]

    def send(ref, send_sem, recv_sem, axis, step):
        copy = remote(ref, ref, send_sem, recv_sem, moved(pos, axis, step))
        copy.start()
        sent.append(copy)

    def arrived(ref, recv_sem):
        remote(ref, ref, recv_sem, recv_sem, moved(pos, "c", 1)).wait_recv()

    offs = (0, -1, 1, 2)

    def onward(j):
        ref = unit(offs[j], 0, every)
        send(ref, bsend.at[f, j, 0], brecv.at[f, j, 0], B, 1)
        send(ref, bsend.at[f, j, 1], brecv.at[f, j, 1], B, -1)
        across(j, 0)

    def across(j, k):
        send(unit(offs[j], offs[k], every), csend.at[f, j, k], crecv.at[f, j, k], "c", 1)

    ref = unit(0, 0, every)
    send(ref, asend.at[f, 0], arecv.at[f, 0], A, 1)
    send(ref, asend.at[f, 1], arecv.at[f, 1], A, -1)
    onward(0)
    yield
    arrived(unit(-1, 0, every), arecv.at[f, 0])
    send(unit(-1, 0, low), asend.at[f, 2], arecv.at[f, 2], A, 1)
    onward(1)
    arrived(unit(1, 0, every), arecv.at[f, 1])
    send(unit(1, 0, high), asend.at[f, 3], arecv.at[f, 3], A, -1)
    onward(2)
    yield

    def relay(j):
        arrived(unit(offs[j], -1, every), brecv.at[f, j, 0])
        send(unit(offs[j], -1, low), bsend.at[f, j, 2], brecv.at[f, j, 2], B, 1)
        across(j, 1)
        arrived(unit(offs[j], 1, every), brecv.at[f, j, 1])
        send(unit(offs[j], 1, high), bsend.at[f, j, 3], brecv.at[f, j, 3], B, -1)
        across(j, 2)

    relay(0)
    yield
    arrived(unit(2, 0, low), arecv.at[f, 2])
    arrived(unit(2, 0, high), arecv.at[f, 3])
    onward(3)
    yield
    relay(1)
    relay(2)
    yield
    relay(3)
    yield
    for j in range(4):
        arrived(unit(offs[j], 2, low), brecv.at[f, j, 2])
        arrived(unit(offs[j], 2, high), brecv.at[f, j, 3])
        across(j, 3)
    yield
    for j in range(4):
        for k in range(4):
            at = {A: lax.rem(a + offs[j] + N, N), B: lax.rem(b + offs[k] + N, N)}
            arrived(full.at[at["x"], at["z"], 1 - c, :, every], crecv.at[f, j, k])
    for copy in sent:
        copy.wait_send()


def run_all(gens):
    gens = list(gens)
    while gens:
        for g in list(gens):
            try:
                next(g)
            except StopIteration:
                gens.remove(g)


def plane_line(pos):
    x, z, y, c = (pos[a] for a in AXES)
    plane = [{"z": lax.rem(z + dz, N), "y": lax.rem(y + dy, N)} for dz in range(N) for dy in range(N) if dz or dy]
    line = [{"x": lax.rem(x + dx, N), "c": lax.rem(c + dc, 2)} for dx in range(N) for dc in range(2) if dx or dc]
    return plane, line


SCATTER = (
    (0, 1280, "x", "z"), (1280, 1280, "z", "x"), (2560, 1280, "x", "z"), (3840, 1280, "z", "x"),
)
NS = len(SCATTER)
W = 1280
TILE = 256
OFF = (0, 1, 3, 5)
FILL = {3: 2, 4: 2, 5: 2, 6: 2, 7: 2}
PIECE = 512


def scatter_chunk(pos, f, gl, w, part, cs, cr, bs, br, keep, ps, pr, out, csem, bsem, psend, precv):
    start, width, A, B = SCATTER[f]
    a, b, c, y = pos[A], pos[B], pos["c"], pos["y"]
    f32, bf16 = jnp.float32, jnp.bfloat16
    part = part.at[f, :, :, :width]
    cs, cr = cs.at[f, :, :, :width], cr.at[f, :, :, :width]
    bs, br = bs.at[f, :, :, :, :width], br.at[f, :, :, :, :width]
    keep, ps, pr = keep.at[f, :, :, :width], ps.at[f, :, :, :, :width], pr.at[f, :, :, :width]
    sent = []

    def index(ia, ib):
        at = {A: ia, B: ib}
        return at["x"] * N + at["z"]

    def shift(p, s):
        return lax.rem(p + s + N, N)

    def send(src, dst, ssem, rsem, device):
        copy = remote(src, dst, ssem, rsem, device)
        copy.start()
        sent.append(copy)

    def arrived(ref, rsem):
        remote(ref, ref, rsem, rsem, moved(pos, "c", 1)).wait_recv()

    def product(i, carry):
        rows = w[pl.ds(pl.multiple_of(start + i * TILE, TILE), TILE), :]
        got = lax.dot_general(
            gl[...].reshape(512, 1024), rows, (((1,), (1,)), ((), ())), preferred_element_type=f32
        )
        some = pl.ds(pl.multiple_of(i * TILE, TILE), TILE)
        cs[:, :, some] = got[:256].reshape(16, 16, TILE).astype(bf16)
        part[:, :, some] = got[256:].reshape(16, 16, TILE)
        return carry

    lax.fori_loop(0, width // TILE, product, 0)
    send(cs, cr, csem.at[0, f], csem.at[1, f], moved(pos, "c", 1))
    yield
    arrived(cr, csem.at[1, f])

    def chip(u):
        return part[u] + cr[u].astype(f32)

    for d in (2, 1, 3):
        def sums(i, carry):
            bs[d - 1, i] = chip(index(i, shift(b, d))).astype(bf16)
            return carry

        lax.fori_loop(0, N, sums, 0)
        send(bs.at[d - 1], br.at[d - 1], bsem.at[0, f, d - 1], bsem.at[1, f, d - 1], moved(pos, B, d))
    yield
    for d in (1, 2, 3):
        arrived(br.at[d - 1], bsem.at[1, f, d - 1])
    for da in (2, 1, 3, 0):
        to = shift(a, da)
        v = chip(index(to, b)) + br[0, to].astype(f32) + br[1, to].astype(f32) + br[2, to].astype(f32)
        for k in range(N):
            ps[da, k] = v[4 * k : 4 * k + 4, :].astype(bf16)
            if da == 0:
                keep[k] = v[4 * k : 4 * k + 4, :]
        for dy in (2, 1, 3, 0):
            if da or dy:
                device = {A: to, "y": shift(y, dy)}
                slot = a * N + y
                send(ps.at[da, shift(y, dy)], pr.at[slot], psend.at[f], precv.at[f], device)
    yield
    group = pr.at[pl.ds(0, 15)]
    arrived(group, precv.at[f])
    mine = a * N + y
    total = keep[y]
    for d in range(1, 16):
        total = total + pr[lax.rem(mine + d, 16)].astype(f32)
    out[:, start : start + width] = total.astype(bf16)
    for copy in sent:
        copy.wait_send()


def step_kernel(h, tl, bl, rr, given, w_hbm, loss, gx, gh,
                tout, tmap, tcon, extra, CH, full, inc, rows, wide, w, L, gl, far_gl, T32, TV, msg, near, mid, far, lmsg, lnear, lmid, lfar,
                part, cs, cr, bs, br, kept_rows, ps, pr, stage,
                wsem, ysend, yrecv, asend, arecv, bsend, brecv, csend, crecv, tsend, trecv, own, zsem, every, pair,
                xsem, rcsem, rbsem, psend, precv, gsem):
    f32, bf16 = jnp.float32, jnp.bfloat16
    pos = spot()
    x, z, y, c = (pos[a] for a in AXES)
    me = ((x * N + z) * N + y) * 2 + c
    plane, line = plane_line(pos)
    loads = []
    for f, (start, width, _, _) in enumerate(CHUNKS):
        copy = pltpu.make_async_copy(w_hbm.at[pl.ds(start, width)], w.at[pl.ds(start, width)], wsem.at[f])
        copy.start()
        loads.append(copy)
    greet(pos, lines(pos, AXES))

    first = []
    for f, (start, width, _, _) in enumerate(CHUNKS):
        cols = pl.ds(start, width)
        for d in (2, 1, 3):
            copy = remote(
                h.at[:, cols], rows.at[y, :, cols], ysend.at[f, d - 1], yrecv.at[f, d - 1], moved(pos, "y", d)
            )
            copy.start()
            first.append(copy)
    for device in lines(pos, ("z",)):
        pl.semaphore_signal(zsem, inc=1, device_id=device, device_id_type=pl.DeviceIdType.MESH)
    rows[y] = h[...]

    def iota(shape, axis):
        return lax.broadcasted_iota(jnp.int32, shape, axis)

    stored = rr[...]
    place = (((stored >> 5) * 2 + ((stored >> 2) & 1)) * 4 + ((stored >> 3) & 3)) * 4 + (stored & 3)
    lane = iota((4, 128), 1)
    mine = jnp.sum(jnp.where(lane == me, place.astype(f32), 0.0), axis=1, keepdims=True)
    here = lane.astype(f32) == mine

    def norms(t):
        v = tl[t].astype(f32)
        top = jnp.max(jnp.max(v, axis=0, keepdims=True), axis=1, keepdims=True)
        total = jnp.sum(jnp.sum(jnp.exp(v - top), axis=0, keepdims=True), axis=1, keepdims=True)
        tcon[t : t + 1] = jnp.where(here[t : t + 1], top + jnp.log(total), -1e30)
        at = jnp.broadcast_to(place[t : t + 1], (128, 128))
        tmap[t] = jnp.where(iota((128, 128), 0) == at, 1.0, 0.0).astype(bf16)

    def slots(t):
        lists = bl[t : t + 1]
        owner = lists >> 3
        held = jnp.where(iota((128, 256), 0) == owner, 1.0, 0.0)
        before = jnp.where(iota((256, 256), 0) < iota((256, 256), 1), 1.0, 0.0).astype(bf16)
        seen = jnp.dot(held.astype(bf16), before, preferred_element_type=f32)
        rank = jnp.sum(held * seen, axis=0, keepdims=True).astype(jnp.int32)
        pick = jnp.where(iota((512, 256), 0) == rank * 128 + owner, 1.0, 0.0).astype(bf16)
        got = jnp.dot(pick, tl[t], preferred_element_type=f32)
        for m in range(MOST):
            T32[pl.ds(t * MOST + m, 128, stride=16), :] = got[128 * m : 128 * m + 128]
        local = jnp.where(owner == me, rank * 8 + (lists & 7), -1)
        kept = jnp.sum(jnp.where(iota((32, 256), 0) == local, 1.0, 0.0), axis=1, keepdims=True)
        CH[t] = jnp.broadcast_to(kept, (32, 128))

    norms(0)
    norms(1)
    gens = []
    for f, (start, width, _, _) in enumerate(CHUNKS):
        cols = pl.ds(start, width)
        for d in (1, 2, 3):
            ref = rows.at[lax.rem(y - d + N, N), :, cols]
            remote(ref, ref, ysend.at[f, d - 1], yrecv.at[f, d - 1], moved(pos, "y", d)).wait_recv()
        for k in range(N):
            wide[4 * k : 4 * k + 4, cols] = rows[k, :, cols].astype(f32)
        full[x, z, c, :, cols] = wide[:, cols].astype(bf16)
        g = gather_chunk(pos, f, full, asend, arecv, bsend, brecv, csend, crecv)
        next(g)
        gens.append(g)
    slots(0)
    slots(1)
    pl.semaphore_wait(zsem, 3)
    for device in lines(pos, ("x",)):
        pl.semaphore_signal(every, inc=1, device_id=device, device_id_type=pl.DeviceIdType.MESH)

    def one(k, carry):
        to = lax.rem(me + k, 128)
        device = {"x": to // 32, "z": lax.rem(to // 8, N), "y": lax.rem(to // 2, N), "c": lax.rem(to, 2)}
        remote(tout.at[to], inc.at[me], tsend, trecv, device).start()
        return carry

    def logits_part(f, lo, hi):
        start, width = CHUNKS[f][:2]

        def tile(i, carry):
            cols = pl.ds(pl.multiple_of(i * TILE, TILE), TILE)
            got = jnp.dot(
                full[:, :, :, :, start : start + width].reshape(512, width),
                w[start : start + width, cols],
                preferred_element_type=f32,
            )
            if f == 0:
                L[:, cols] = got
            else:
                L[:, cols] += got
            return carry

        lax.fori_loop(lo, hi, tile, 0)

    def finish(g):
        for _ in g:
            pass

    g0, g1, g2, g3 = gens
    next(g0), next(g1)
    next(g2), next(g3)
    slots(2)
    next(g0), next(g1)
    slots(3)
    next(g2), next(g3)
    norms(2)
    norms(3)
    pl.semaphore_wait(every, 3)
    pl.semaphore_signal(pair, inc=1, device_id=moved(pos, "c", 1), device_id_type=pl.DeviceIdType.MESH)
    next(g0), next(g1)
    tout[...] = T32[...].reshape(128, 16, 128).astype(bf16)
    keep = pltpu.make_async_copy(tout.at[me], inc.at[me], own.at[0])
    keep.start()
    pl.semaphore_wait(pair, 1)
    next(g2), next(g3)
    next(g0), next(g1)
    natural = iota((128, 128), 1)
    natural = (natural >> 5) * 32 + ((natural >> 2) & 3) * 8 + ((natural >> 4) & 1) * 4 + (natural & 3)
    turn = jnp.where(iota((128, 128), 0) == natural, 1.0, 0.0)
    extra[...] = jnp.dot(given[...], turn, preferred_element_type=f32, precision=lax.Precision.HIGHEST)
    next(g2), next(g3)
    next(g0), next(g1)
    finish(g0)
    next(g2), next(g3)
    loads[0].wait()
    logits_part(0, 0, 2)
    next(g2), next(g3)
    lax.fori_loop(1, 128, one, 0)
    logits_part(0, 2, 4)
    finish(g1)
    loads[1].wait()
    logits_part(1, 0, 4)
    finish(g2)
    loads[2].wait()
    logits_part(2, 0, 4)
    finish(g3)
    loads[3].wait()
    logits_part(3, 0, 4)
    for copy in first:
        copy.wait_send()

    for t in range(N):
        r = slice(128 * t, 128 * t + 128)
        top = L[r, :128]
        for b in range(1, 8):
            top = jnp.maximum(top, L[r, 128 * b : 128 * b + 128])
        col = jnp.max(top, axis=1, keepdims=True)
        acc = jnp.exp(L[r, :128] - col)
        for b in range(1, 8):
            acc = acc + jnp.exp(L[r, 128 * b : 128 * b + 128] - col)
        msg[0, t : t + 1] = jnp.max(top.T, axis=0, keepdims=True)
        msg[1, t : t + 1] = jnp.sum(acc.T, axis=0, keepdims=True)
    msg[0, 4:8] = tcon[0:4]
    msg[1, 4:8] = jnp.zeros((4, 128), f32)

    def merge(parts):
        top = parts[0][0]
        for p in parts[1:]:
            top = jnp.maximum(top, p[0])
        total = 0.0
        for p in parts:
            total += p[1] * jnp.exp(p[0] - top)
        return top, total

    for device in plane:
        remote(msg, near.at[z * N + y], xsem.at[0], xsem.at[1], device).start()
    near[z * N + y] = msg[...]

    part_inc = inc.at[pl.ds(0, 127)]
    remote(part_inc, part_inc, tsend, trecv, moved(pos, "c", 1)).wait()
    keep.wait()
    T32[...] = inc[...].reshape(2048, 128).astype(f32)

    def teacher(t):
        stored = jnp.concatenate(
            [T32[pl.ds(t * MOST + m, 128, stride=16), :] for m in range(MOST)], axis=1
        ).astype(bf16)
        ordered = jnp.dot(tmap[t], stored, preferred_element_type=f32)
        for b in range(8):
            v = CH[t, b : b + 1] * ordered[:, :128]
            for m in range(1, MOST):
                v = v + CH[t, m * 8 + b : m * 8 + b + 1] * ordered[:, 128 * m : 128 * m + 128]
            TV[t, b] = v.astype(bf16)

    teacher(0)
    teacher(1)
    group = near.at[pl.ds(0, 15)]
    remote(group, group, xsem.at[0], xsem.at[1], plane[0]).wait()
    mid[0], mid[1] = merge([near[i] for i in range(16)])
    for device in line:
        remote(mid, far.at[x * 2 + c], xsem.at[2], xsem.at[3], device).start()
    far[x * 2 + c] = mid[...]
    teacher(2)
    teacher(3)
    group = far.at[pl.ds(0, 7)]
    remote(group, group, xsem.at[2], xsem.at[3], line[0]).wait()
    top, total = merge([far[i] for i in range(8)])

    log_norm = top[0:4] + jnp.log(total[0:4])
    tail = extra[0:4]
    weight = extra[4:8]
    kept = jnp.log(1.0 - tail) - top[4:8]
    tail_prob = tail / UNLISTED
    tail_log = jnp.log(tail_prob)

    def column(v, t):
        return jnp.broadcast_to(v[t : t + 1], (128, 128)).T

    lmsg[...] = jnp.zeros((8, 128), f32)
    for t in range(N):
        r = slice(128 * t, 128 * t + 128)
        norm_c, weight_c, kept_c = column(log_norm, t), column(weight, t), column(kept, t)
        prob_c, log_c = column(tail_prob, t), column(tail_log, t)
        acc = jnp.zeros((128, 128), f32)
        for b in range(8):
            scores = L[r, 128 * b : 128 * b + 128]
            on = CH[t, b : b + 1] + CH[t, 8 + b : 9 + b] + CH[t, 16 + b : 17 + b] + CH[t, 24 + b : 25 + b]
            off = 1.0 - on
            listed_log = TV[t, b].astype(f32) + kept_c
            q = on * jnp.exp(listed_log) + off * prob_c
            log_q = on * listed_log + off * log_c
            gap = scores - norm_c
            g = (weight_c * (jnp.exp(gap) - q)).astype(bf16)
            gl[r, 128 * b : 128 * b + 128] = g
            g = g.reshape(4, 2, 16, 128)
            far_gl[c, 4 * t : 4 * t + 4, :, 128 * b : 128 * b + 128] = g[:, 1]
            far_gl[1 - c, 4 * t : 4 * t + 4, :, 128 * b : 128 * b + 128] = g[:, 0]
            acc = acc + q * (log_q - gap)
        lmsg[t : t + 1] = jnp.sum(acc.T, axis=0, keepdims=True)

    stores = [None, None]
    count = [0]

    def head_pieces(n):
        lo = count[0]
        count[0] = lo + n

        def piece(i, carry):
            some = pl.ds(pl.multiple_of(i * PIECE, PIECE), PIECE)
            gh[some, :] = lax.dot_general(
                full[:, :, :, :, some].reshape(512, PIECE), gl[...], (((0,), (0,)), ((), ())),
                preferred_element_type=f32,
            ).astype(bf16)
            return carry

        lax.fori_loop(lo, lo + n, piece, 0)

    chunks = [
        scatter_chunk(pos, f, far_gl, w, part, cs, cr, bs, br, kept_rows, ps, pr, gx, rcsem, rbsem, psend, precv)
        for f in range(NS)
    ]
    for tick in range(NS + OFF[-1]):
        for f in range(NS):
            if tick - f in OFF:
                next(chunks[f], None)
        if tick == 0:
            for device in plane:
                remote(lmsg, lnear.at[z * N + y], xsem.at[4], xsem.at[5], device).start()
            lnear[z * N + y] = lmsg[...]
        if tick == OFF[1] + 3:
            group = lnear.at[pl.ds(0, 15)]
            remote(group, group, xsem.at[4], xsem.at[5], plane[0]).wait()
            total = lnear[0]
            for i in range(1, 16):
                total = total + lnear[i]
            lmid[...] = total
            for device in line:
                remote(lmid, lfar.at[x * 2 + c], xsem.at[6], xsem.at[7], device).start()
            lfar[x * 2 + c] = lmid[...]
        if tick in FILL:
            head_pieces(FILL[tick])
    group = lfar.at[pl.ds(0, 7)]
    remote(group, group, xsem.at[6], xsem.at[7], line[0]).wait()
    total = lfar[0]
    for i in range(1, 8):
        total = total + lfar[i]
    loss[...] = total


UNLISTED = 98304.0


def step(hidden, teacher, lists, reader, given, head):
    bf16, f32 = jnp.bfloat16, jnp.float32
    V = pltpu.VMEM
    return pl.pallas_call(
        step_kernel,
        out_shape=(
            jax.ShapeDtypeStruct((8, 128), f32),
            jax.ShapeDtypeStruct((4, D), bf16),
            pltpu.VMEM(head.shape, bf16),
        ),
        in_specs=[VM, VM, VM, VM, VM, ANY],
        out_specs=(VM, VM, VM),
        scratch_shapes=[
            V((128, 16, 128), bf16), V((N, 128, 128), bf16), V((N, 128), f32), V((8, 128), f32), V((N, 32, 128), f32),
            V((N, N, 2, 16, D), bf16),
            V((128, 16, 128), bf16),
            V((N, 4, D), bf16),
            V((16, D), f32),
            V(head.shape, bf16),
            V((512, 1024), f32),
            V((512, 1024), bf16),
            V((2, 16, 16, 1024), bf16),
            V((2048, 128), f32),
            V((N, 8, 128, 128), bf16),
            V((2, 8, 128), f32), V((16, 2, 8, 128), f32), V((2, 8, 128), f32), V((8, 2, 8, 128), f32),
            V((8, 128), f32), V((16, 8, 128), f32), V((8, 128), f32), V((8, 8, 128), f32),
            V((NS, 16, 16, W), f32),
            V((NS, 16, 16, W), bf16), V((NS, 16, 16, W), bf16),
            V((NS, 3, N, 16, W), bf16), V((NS, 3, N, 16, W), bf16),
            V((NS, N, 4, W), f32),
            V((NS, N, N, 4, W), bf16), V((NS, 16, 4, W), bf16),
            V((8, 128), bf16),
            DMA((NC,)),
            DMA((NC, 3)), DMA((NC, 3)),
            DMA((NC, 4)), DMA((NC, 4)),
            DMA((NC, 4, 4)), DMA((NC, 4, 4)),
            DMA((NC, 4, 4)), DMA((NC, 4, 4)),
            DMA, DMA, DMA((2,)), REGULAR, REGULAR, REGULAR,
            DMA((8,)),
            DMA((2, NS)), DMA((2, NS, 3)), DMA((NS,)), DMA((NS,)), DMA((2,)),
        ],
        compiler_params=pltpu.CompilerParams(collective_id=0, has_side_effects=True, vmem_limit_bytes=53 << 20),
        name="step",
    )(hidden, teacher, lists, reader, given, head)


def on_device(
    hidden_states, head_weight, teacher_logits, block_lists, row_reader, tail_mass, token_weight
):
    x, z, y, c = (lax.axis_index(a) for a in AXES)
    given = jnp.concatenate([tail_mass.reshape(N, 128), token_weight.reshape(N, 128)])
    row_loss, grad_hidden, grad_head = step(
        hidden_states, teacher_logits[:, :, 0, :], block_lists, row_reader, given, head_weight
    )
    token_loss = lax.dynamic_slice(row_loss, (x, (z * 2 + c) * 16 + y * 4), (1, 4)).reshape(4)
    return (token_loss, grad_head, grad_hidden)


def solution(mesh):
    split = Mesh(mesh.devices.reshape(N, N, N, 2), AXES)
    return jax.shard_map(
        on_device,
        mesh=split,
        in_specs=(P(AXES, None), P(None, AXES), P(None, None, AXES, None), P(), P(), P(), P()),
        out_specs=(P(AXES), P(None, AXES), P(AXES, None)),
        check_vma=False,
    )
```

time: 120 us -> 101 us (0.84)
  local copies, waits for them, and re-layouts: 15.5 us -> 5.98 us
  other arithmetic: 6.88 us -> 1.3 us
  Pallas kernels: 95.5 us -> 92.7 us
  matrix products: 1.43 us -> 0 us
    unnamed x4, local copies, waits for them, and re-layouts: 9.94 us -> 4.71 us
    reshape x7 -> x0, local copies, waits for them, and re-layouts: 4.08 us -> none  [the longest x4 1.88 us: arranged(): v.reshape(blocks, N, N, 2, 4).transpose(0, 1, 3, 2, 4)]
    pallas_call x1, Pallas kernels: 95.5 us -> 92.7 us  [step(): pl.pallas_call(step_kernel, out_shape=(jax.ShapeDtypeStruct((8, 128), f32...]
    reduce_sum x3 -> x0, other arithmetic: 1.72 us -> none  [the longest x1 1.21 us: on_device(): jnp.sum(jnp.exp(stored - stored_max[:, None, None]), axis=(1, 2))]
    dot_general x1 -> x0, matrix products: 1.43 us -> none  [on_device(): jnp.einsum('tsk,tkc->tsc', picker, teacher_logits[:, :, 0, :], preferred_...]
where the time goes in v3:
time: 101 us
  Pallas kernels  92.7 us (92%)
  local copies, waits for them, and re-layouts  5.98 us (6%)
  other arithmetic  1.3 us (1%)
    pallas_call x1, Pallas kernels, step(): pl.pallas_call(step_kernel, out_shape=(jax.ShapeDtypeStruct((8, 128), f32...  92.7 us
    unnamed x4, local copies, waits for them, and re-layouts  4.71 us

profile of v3, /device:TPU:0, one launch (start us, length us, event | category | flops | bytes accessed | tf_op | source)
XLA Modules:
  0.0 100.6 jit_solution(5981873982933061700)
XLA Ops:
  0.6 1.3 %pad_maximum_fusion.given = f32[8,128]{1,0:T(8,128)} fusion(f32[4,128]{1,0:T(4,128)} %bitcast.6, f32[4,128]{1,0:T(4,128)} %bitcast.7), kind=kLoop, calls=%fused_computation | loop fusion | flops 1024 | bytes 8192 | tf_op jit(solution)/shard_map/concatenate | solution.py:575
  1.9 92.7 %step.1 = (f32[8,128]{1,0:T(8,128)}, bf16[4,5120]{1,0:T(4,128)(2,1)}, bf16[5120,1024]{1,0:T(8,128)(2,1)S(1)}) custom-call(bf16[4,5120]{1,0:T(4,128)(2,1)} %h.1, bf16[4,256,128]{2,1,0:T(8,128)(2,1)} %bitcast.5, s32[4,256]{1,0:T(4,128)} %bl.1, s32[4,128]{1,0:T(4,128)} %rr.1, f32[8,128]{1,0:T(8,128)} %pad_maximum_fusion.given, bf16[5120,1024]{1,0:T(8,128)(2,1)} %w_hbm.1), custom_call_target="tpu_custom_call" | custom-call | tf_op jit(solution)/shard_map/step/pallas_call | solution.py:528
  94.6 1.3 %dynamic-slice_bitcast_fusion = f32[4]{0:T(128)} fusion(f32[8,128]{1,0:T(8,128)} %get-tuple-element.6, s32[]{:T(128)S(6)} %select_n.6, s32[]{:T(128)S(6)} %select_n.7), kind=kLoop, calls=%fused_computation.1 | loop fusion | bytes 40 | tf_op jit(solution)/shard_map/reshape | solution.py:579
  95.9 0.0 copy-start
  95.9 4.1 %copy.12 = bf16[5120,1024]{1,0:T(8,128)(2,1)} copy(bf16[5120,1024]{1,0:T(8,128)(2,1)S(1)} %get-tuple-element.10) | data formatting | bytes 20971520
  100.0 0.0 copy-done
  100.0 0.6 copy.13
Async XLA Ops:
  95.9 4.1 %copy-start = (bf16[4,5120]{1,0:T(4,128)(2,1)S(1)}, bf16[4,5120]{1,0:T(4,128)(2,1)}, u32[]{:S(2)}) copy-start(bf16[4,5120]{1,0:T(4,128)(2,1)} %get-tuple-element.17) | copy-start | bytes 122884

commit v4 on v3

--- a/solution.py
+++ b/solution.py
@@ -141,23 +141,26 @@
 
 
 SCATTER = (
-    (0, 1280, "x", "z"), (1280, 1280, "z", "x"), (2560, 1280, "x", "z"), (3840, 1280, "z", "x"),
+    (0, 768, ("x", "y"), "z"), (768, 768, ("z", "y"), "x"), (1536, 768, ("x", "z"), "y"),
+    (2304, 1024, ("x", "y"), "z"), (3328, 1024, ("z", "y"), "x"), (4352, 768, ("x", "z"), "y"),
 )
 NS = len(SCATTER)
-W = 1280
+W = 1024
+WY = 768
 TILE = 256
-OFF = (0, 1, 3, 5)
-FILL = {3: 2, 4: 2, 5: 2, 6: 2, 7: 2}
 PIECE = 512
-
-
-def scatter_chunk(pos, f, gl, w, part, cs, cr, bs, br, keep, ps, pr, out, csem, bsem, psend, precv):
-    start, width, A, B = SCATTER[f]
-    a, b, c, y = pos[A], pos[B], pos["c"], pos["y"]
+OFF = (0, 1, 4, 7)
+FILL = {6: 2, 7: 2, 8: 2, 9: 2, 10: 2}
+
+
+def scatter_chunk(pos, f, gl, w, part, cs, cr, bs, br, bsy, bry, keep, ps, pr, out, csem, bsem, psend, precv):
+    start, width, (A, A2), B = SCATTER[f]
+    a, a2, b, c, y = pos[A], pos[A2], pos[B], pos["c"], pos["y"]
     f32, bf16 = jnp.float32, jnp.bfloat16
     part = part.at[f, :, :, :width]
     cs, cr = cs.at[f, :, :, :width], cr.at[f, :, :, :width]
     bs, br = bs.at[f, :, :, :, :width], br.at[f, :, :, :, :width]
+    bsy, bry = bsy.at[f // 3], bry.at[f // 3]
     keep, ps, pr = keep.at[f, :, :, :width], ps.at[f, :, :, :, :width], pr.at[f, :, :, :width]
     sent = []
 
@@ -166,7 +169,7 @@
         return at["x"] * N + at["z"]
 
     def shift(p, s):
-        return lax.rem(p + s + N, N)
+        return lax.rem(p + s, N)
 
     def send(src, dst, ssem, rsem, device):
         copy = remote(src, dst, ssem, rsem, device)
@@ -194,33 +197,62 @@
     def chip(u):
         return part[u] + cr[u].astype(f32)
 
-    for d in (2, 1, 3):
-        def sums(i, carry):
-            bs[d - 1, i] = chip(index(i, shift(b, d))).astype(bf16)
+    def offer(da, d2, ref):
+        device = {A: shift(a, da), A2: shift(a2, d2)}
+        send(ref, pr.at[a * N + a2], psend.at[f], precv.at[f], device)
+
+    if B == "y":
+        def rows_of(u, carry):
+            v = chip(u)
+            for k in range(N):
+                bsy[k, u] = v[4 * k : 4 * k + 4, :].astype(bf16)
             return carry
 
-        lax.fori_loop(0, N, sums, 0)
-        send(bs.at[d - 1], br.at[d - 1], bsem.at[0, f, d - 1], bsem.at[1, f, d - 1], moved(pos, B, d))
-    yield
-    for d in (1, 2, 3):
-        arrived(br.at[d - 1], bsem.at[1, f, d - 1])
-    for da in (2, 1, 3, 0):
-        to = shift(a, da)
-        v = chip(index(to, b)) + br[0, to].astype(f32) + br[1, to].astype(f32) + br[2, to].astype(f32)
-        for k in range(N):
-            ps[da, k] = v[4 * k : 4 * k + 4, :].astype(bf16)
-            if da == 0:
-                keep[k] = v[4 * k : 4 * k + 4, :]
-        for dy in (2, 1, 3, 0):
-            if da or dy:
-                device = {A: to, "y": shift(y, dy)}
-                slot = a * N + y
-                send(ps.at[da, shift(y, dy)], pr.at[slot], psend.at[f], precv.at[f], device)
+        lax.fori_loop(0, 16, rows_of, 0)
+        for d in (2, 1, 3):
+            send(bsy.at[shift(y, d)], bry.at[d - 1], bsem.at[0, f, d - 1], bsem.at[1, f, d - 1], moved(pos, "y", d))
+        yield
+        for d in (1, 2, 3):
+            arrived(bry.at[d - 1], bsem.at[1, f, d - 1])
+
+        def line_sum(u):
+            v = bsy[y, u].astype(f32) + bry[0, u].astype(f32)
+            return v + bry[1, u].astype(f32) + bry[2, u].astype(f32)
+
+        for da in (2, 1, 3, 0):
+            for d2 in (2, 1, 3, 0):
+                v = line_sum(shift(a, da) * N + shift(a2, d2))
+                if da or d2:
+                    ps[da, d2] = v.astype(bf16)
+                    offer(da, d2, ps.at[da, d2])
+                else:
+                    keep[0] = v
+    else:
+        for d in (2, 1, 3):
+            def sums(i, carry):
+                bs[d - 1, i] = chip(index(i, shift(b, d))).astype(bf16)
+                return carry
+
+            lax.fori_loop(0, N, sums, 0)
+            send(bs.at[d - 1], br.at[d - 1], bsem.at[0, f, d - 1], bsem.at[1, f, d - 1], moved(pos, B, d))
+        yield
+        for d in (1, 2, 3):
+            arrived(br.at[d - 1], bsem.at[1, f, d - 1])
+        for da in (2, 1, 3, 0):
+            to = shift(a, da)
+            v = chip(index(to, b)) + br[0, to].astype(f32) + br[1, to].astype(f32) + br[2, to].astype(f32)
+            for k in range(N):
+                ps[da, k] = v[4 * k : 4 * k + 4, :].astype(bf16)
+                if da == 0:
+                    keep[k] = v[4 * k : 4 * k + 4, :]
+            for d2 in (2, 1, 3, 0):
+                if da or d2:
+                    offer(da, d2, ps.at[da, shift(y, d2)])
     yield
     group = pr.at[pl.ds(0, 15)]
     arrived(group, precv.at[f])
-    mine = a * N + y
-    total = keep[y]
+    mine = a * N + a2
+    total = keep[0] if B == "y" else keep[y]
     for d in range(1, 16):
         total = total + pr[lax.rem(mine + d, 16)].astype(f32)
     out[:, start : start + width] = total.astype(bf16)
@@ -228,9 +260,9 @@
         copy.wait_send()
 
 
-def step_kernel(h, tl, bl, rr, given, w_hbm, loss, gx, gh,
+def step_kernel(h, tl, bl, rr, tail_in, weight_in, w_hbm, loss, gx, gh,
                 tout, tmap, tcon, extra, CH, full, inc, rows, wide, w, L, gl, far_gl, T32, TV, msg, near, mid, far, lmsg, lnear, lmid, lfar,
-                part, cs, cr, bs, br, kept_rows, ps, pr, stage,
+                part, cs, cr, bs, br, bsy, bry, kept_rows, ps, pr, stage,
                 wsem, ysend, yrecv, asend, arecv, bsend, brecv, csend, crecv, tsend, trecv, own, zsem, every, pair,
                 xsem, rcsem, rbsem, psend, precv, gsem):
     f32, bf16 = jnp.float32, jnp.bfloat16
@@ -359,7 +391,9 @@
     natural = iota((128, 128), 1)
     natural = (natural >> 5) * 32 + ((natural >> 2) & 3) * 8 + ((natural >> 4) & 1) * 4 + (natural & 3)
     turn = jnp.where(iota((128, 128), 0) == natural, 1.0, 0.0)
-    extra[...] = jnp.dot(given[...], turn, preferred_element_type=f32, precision=lax.Precision.HIGHEST)
+    extra[0:4] = tail_in[...]
+    extra[4:8] = weight_in[...]
+    extra[...] = jnp.dot(extra[...], turn, preferred_element_type=f32, precision=lax.Precision.HIGHEST)
     next(g2), next(g3)
     next(g0), next(g1)
     finish(g0)
@@ -488,11 +522,11 @@
         lax.fori_loop(lo, lo + n, piece, 0)
 
     chunks = [
-        scatter_chunk(pos, f, far_gl, w, part, cs, cr, bs, br, kept_rows, ps, pr, gx, rcsem, rbsem, psend, precv)
+        scatter_chunk(pos, f, far_gl, w, part, cs, cr, bs, br, bsy, bry, kept_rows, ps, pr, gx, rcsem, rbsem, psend, precv)
         for f in range(NS)
     ]
     for tick in range(NS + OFF[-1]):
-        for f in range(NS):
+        for f in reversed(range(NS)):
             if tick - f in OFF:
                 next(chunks[f], None)
         if tick == 0:
@@ -516,13 +550,18 @@
     total = lfar[0]
     for i in range(1, 8):
         total = total + lfar[i]
-    loss[...] = total
+    row = jnp.sum(jnp.where(iota((8, 128), 0) == x, total, 0.0), axis=0, keepdims=True)
+    lanes = iota((128, 128), 1)
+    pick = jnp.where((iota((128, 128), 0) == (z * 2 + c) * 16 + y * 4 + lanes) & (lanes < 4), 1.0, 0.0)
+    loss[...] = jnp.dot(
+        jnp.broadcast_to(row, (8, 128)), pick, preferred_element_type=f32, precision=lax.Precision.HIGHEST
+    )
 
 
 UNLISTED = 98304.0
 
 
-def step(hidden, teacher, lists, reader, given, head):
+def step(hidden, teacher, lists, reader, tail, weight, head):
     bf16, f32 = jnp.bfloat16, jnp.float32
     V = pltpu.VMEM
     return pl.pallas_call(
@@ -532,7 +571,7 @@
             jax.ShapeDtypeStruct((4, D), bf16),
             pltpu.VMEM(head.shape, bf16),
         ),
-        in_specs=[VM, VM, VM, VM, VM, ANY],
+        in_specs=[VM, VM, VM, VM, VM, VM, ANY],
         out_specs=(VM, VM, VM),
         scratch_shapes=[
             V((128, 16, 128), bf16), V((N, 128, 128), bf16), V((N, 128), f32), V((8, 128), f32), V((N, 32, 128), f32),
@@ -551,6 +590,7 @@
             V((NS, 16, 16, W), f32),
             V((NS, 16, 16, W), bf16), V((NS, 16, 16, W), bf16),
             V((NS, 3, N, 16, W), bf16), V((NS, 3, N, 16, W), bf16),
+            V((2, N, 16, 4, WY), bf16), V((2, 3, 16, 4, WY), bf16),
             V((NS, N, 4, W), f32),
             V((NS, N, N, 4, W), bf16), V((NS, 16, 4, W), bf16),
             V((8, 128), bf16),
@@ -565,18 +605,16 @@
         ],
         compiler_params=pltpu.CompilerParams(collective_id=0, has_side_effects=True, vmem_limit_bytes=53 << 20),
         name="step",
-    )(hidden, teacher, lists, reader, given, head)
+    )(hidden, teacher, lists, reader, tail, weight, head)
 
 
 def on_device(
     hidden_states, head_weight, teacher_logits, block_lists, row_reader, tail_mass, token_weight
 ):
-    x, z, y, c = (lax.axis_index(a) for a in AXES)
-    given = jnp.concatenate([tail_mass.reshape(N, 128), token_weight.reshape(N, 128)])
     row_loss, grad_hidden, grad_head = step(
-        hidden_states, teacher_logits[:, :, 0, :], block_lists, row_reader, given, head_weight
+        hidden_states, teacher_logits[:, :, 0, :], block_lists, row_reader, tail_mass.reshape(N, 128), token_weight.reshape(N, 128), head_weight
     )
-    token_loss = lax.dynamic_slice(row_loss, (x, (z * 2 + c) * 16 + y * 4), (1, 4)).reshape(4)
+    token_loss = row_loss[0, :4]
     return (token_loss, grad_head, grad_hidden)
 
 

time: 101 us -> 92 us (0.911)
  Pallas kernels: 92.7 us -> 85.1 us
  other arithmetic: 1.3 us -> 0 us
    pallas_call x1, Pallas kernels: 92.7 us -> 85.1 us  [step(): pl.pallas_call(step_kernel, out_shape=(jax.ShapeDtypeStruct((8, 128), f32...]
    concatenate x1 -> x0, other arithmetic: 1.3 us -> none  [on_device(): jnp.concatenate([tail_mass.reshape(N, 128), token_weight.reshape(N, 128)])]
    reshape x1 -> x0, local copies, waits for them, and re-layouts: 1.27 us -> none  [on_device(): lax.dynamic_slice(row_loss, (x, (z * 2 + c) * 16 + y * 4), (1, 4))]
    squeeze x0 -> x1, local copies, waits for them, and re-layouts: none -> 1.19 us  [on_device(): token_loss = row_loss[0, :4]]
where the time goes in v4:
time: 92 us; the launch traced here: 91.6 us
  Pallas kernels  85.1 us (92%)
  local copies, waits for them, and re-layouts  5.9 us (6%)
    pallas_call x1, Pallas kernels, step(): pl.pallas_call(step_kernel, out_shape=(jax.ShapeDtypeStruct((8, 128), f32...  85.1 us
    unnamed x4, local copies, waits for them, and re-layouts  4.71 us

profile of v4, /device:TPU:0, one launch (start us, length us, event | category | flops | bytes accessed | tf_op | source)
XLA Modules:
  0.0 91.6 jit_solution(6331570371998153482)
XLA Ops:
  0.6 85.1 %step.1 = (f32[8,128]{1,0:T(8,128)}, bf16[4,5120]{1,0:T(4,128)(2,1)}, bf16[5120,1024]{1,0:T(8,128)(2,1)S(1)}) custom-call(bf16[4,5120]{1,0:T(4,128)(2,1)} %h.1, bf16[4,256,128]{2,1,0:T(8,128)(2,1)} %bitcast.5, s32[4,256]{1,0:T(4,128)} %bl.1, s32[4,128]{1,0:T(4,128)} %rr.1, f32[4,128]{1,0:T(4,128)} %bitcast.6, f32[4,128]{1,0:T(4,128)} %bitcast.7, ...), custom_call_target="tpu_custom_call" | custom-call | tf_op jit(solution)/shard_map/step/pallas_call | solution.py:567
  85.7 1.2 %slice_bitcast_fusion = f32[4]{0:T(128)} fusion(f32[8,128]{1,0:T(8,128)} %get-tuple-element.6), kind=kLoop, calls=%fused_computation | loop fusion | bytes 32 | tf_op jit(solution)/shard_map/squeeze | solution.py:617
  86.9 0.0 copy-start
  86.9 4.1 %copy.12 = bf16[5120,1024]{1,0:T(8,128)(2,1)} copy(bf16[5120,1024]{1,0:T(8,128)(2,1)S(1)} %get-tuple-element.10) | data formatting | bytes 20971520
  91.0 0.0 copy-done
  91.0 0.6 copy.13
Async XLA Ops:
  86.9 4.1 %copy-start = (bf16[4,5120]{1,0:T(4,128)(2,1)S(1)}, bf16[4,5120]{1,0:T(4,128)(2,1)}, u32[]{:S(2)}) copy-start(bf16[4,5120]{1,0:T(4,128)(2,1)} %get-tuple-element.17) | copy-start | bytes 122884

commit v5 on v4

--- a/solution.py
+++ b/solution.py
@@ -396,13 +396,12 @@
     extra[...] = jnp.dot(extra[...], turn, preferred_element_type=f32, precision=lax.Precision.HIGHEST)
     next(g2), next(g3)
     next(g0), next(g1)
+    next(g2), next(g3)
     finish(g0)
     next(g2), next(g3)
+    lax.fori_loop(1, 128, one, 0)
     loads[0].wait()
-    logits_part(0, 0, 2)
-    next(g2), next(g3)
-    lax.fori_loop(1, 128, one, 0)
-    logits_part(0, 2, 4)
+    logits_part(0, 0, 4)
     finish(g1)
     loads[1].wait()
     logits_part(1, 0, 4)

time: 92 us -> 90.2 us (0.980)
  Pallas kernels: 85.1 us -> 83.3 us
    pallas_call x1, Pallas kernels: 85.1 us -> 83.3 us  [step(): pl.pallas_call(step_kernel, out_shape=(jax.ShapeDtypeStruct((8, 128), f32...]
where the time goes in v5:
time: 90.2 us; the launch traced here: 89.8 us
  Pallas kernels  83.3 us (92%)
  local copies, waits for them, and re-layouts  5.9 us (7%)
    pallas_call x1, Pallas kernels, step(): pl.pallas_call(step_kernel, out_shape=(jax.ShapeDtypeStruct((8, 128), f32...  83.3 us
    unnamed x4, local copies, waits for them, and re-layouts  4.71 us

profile of v5, /device:TPU:0, one launch (start us, length us, event | category | flops | bytes accessed | tf_op | source)
XLA Modules:
  0.0 89.8 jit_solution(12115109688442201738)
XLA Ops:
  0.6 83.3 %step.1 = (f32[8,128]{1,0:T(8,128)}, bf16[4,5120]{1,0:T(4,128)(2,1)}, bf16[5120,1024]{1,0:T(8,128)(2,1)S(1)}) custom-call(bf16[4,5120]{1,0:T(4,128)(2,1)} %h.1, bf16[4,256,128]{2,1,0:T(8,128)(2,1)} %bitcast.5, s32[4,256]{1,0:T(4,128)} %bl.1, s32[4,128]{1,0:T(4,128)} %rr.1, f32[4,128]{1,0:T(4,128)} %bitcast.6, f32[4,128]{1,0:T(4,128)} %bitcast.7, ...), custom_call_target="tpu_custom_call" | custom-call | tf_op jit(solution)/shard_map/step/pallas_call | solution.py:566
  83.9 1.2 %slice_bitcast_fusion = f32[4]{0:T(128)} fusion(f32[8,128]{1,0:T(8,128)} %get-tuple-element.6), kind=kLoop, calls=%fused_computation | loop fusion | bytes 32 | tf_op jit(solution)/shard_map/squeeze | solution.py:616
  85.1 0.0 copy-start
  85.1 4.1 %copy.12 = bf16[5120,1024]{1,0:T(8,128)(2,1)} copy(bf16[5120,1024]{1,0:T(8,128)(2,1)S(1)} %get-tuple-element.10) | data formatting | bytes 20971520
  89.2 0.0 copy-done
  89.2 0.6 copy.13
Async XLA Ops:
  85.1 4.1 %copy-start = (bf16[4,5120]{1,0:T(4,128)(2,1)S(1)}, bf16[4,5120]{1,0:T(4,128)(2,1)}, u32[]{:S(2)}) copy-start(bf16[4,5120]{1,0:T(4,128)(2,1)} %get-tuple-element.17) | copy-start | bytes 122884
